TPU v7x, 512 devices: a whole 4x8x8 slice. The times are simulated.
512 devices in a mesh: wl: 16 (over y, core), sec: 32 (over x, z).
Axes of the slice: x: 4, y: 8, z: 8, core: 2. Of those that a mesh axis runs over, the one named last changes fastest.
Arguments:
- sections: float32 [128, 32, 2, 2, 128, 128], P('sec', None, None, None, 'wl'), as said below
- launch_mode: int32 [32], P('wl'), may hold values from 0 to 127
Outputs:
- forward_field: float32 [128, 32, 2, 128], P('sec', 'wl')
- backward_field: float32 [128, 32, 2, 128], P('sec', 'wl')
Inputs may be any that keep to these rules, and one draw needn't show every extreme that they name: `sections`: every entry is finite; each matrix is a unit-modulus diagonal plus a full coupling, scaled so that it keeps a field's power on average.
All inputs are finite; a program needn't handle non-finite values.
Results may differ from a plain program's by a relative error of at most 0.0003.
Values sent between devices are 32-bit elements; how exact they have to be, the bound alone decides.
No kernel may reach another device: no remote copies, remote signals or barrier semaphores. Data moves between devices by JAX's collectives and lax.ppermute only.
A program may use at most 64 MiB of HBM per device.

v0:
```python
import math

import jax
import jax.numpy as jnp
from jax import lax
from jax.sharding import PartitionSpec as P


def entering(part, axis, combine, identity, reverse):
    count = lax.axis_size(axis)
    place = lax.axis_index(axis)
    ahead = count - 1 - place if reverse else place
    gathered = lax.all_gather(part, axis)
    state = jnp.zeros_like(part) + jnp.asarray(identity, part.dtype)

    def one(turn, state):
        source = count - 1 - turn if reverse else turn
        return combine(state, lax.dynamic_index_in_dim(gathered, source, 0, False))

    return lax.fori_loop(0, ahead, one, state)


def matrix_product(outer_mat, inner_mat):
    return jnp.matmul(outer_mat, inner_mat, precision=lax.Precision.HIGHEST)


def complex_product(outer_mat, inner_mat):
    real_part = matrix_product(outer_mat[..., 0, :, :], inner_mat[..., 0, :, :]) - matrix_product(
        outer_mat[..., 1, :, :], inner_mat[..., 1, :, :]
    )
    imag_part = matrix_product(outer_mat[..., 0, :, :], inner_mat[..., 1, :, :]) + matrix_product(
        outer_mat[..., 1, :, :], inner_mat[..., 0, :, :]
    )
    return jnp.stack([real_part, imag_part], axis=-3)


def complex_apply(matrix, vector):
    real_part = jnp.einsum(
        "...ij,...j->...i", matrix[..., 0, :, :], vector[..., 0, :], precision=lax.Precision.HIGHEST
    ) - jnp.einsum(
        "...ij,...j->...i", matrix[..., 1, :, :], vector[..., 1, :], precision=lax.Precision.HIGHEST
    )
    imag_part = jnp.einsum(
        "...ij,...j->...i", matrix[..., 0, :, :], vector[..., 1, :], precision=lax.Precision.HIGHEST
    ) + jnp.einsum(
        "...ij,...j->...i", matrix[..., 1, :, :], vector[..., 0, :], precision=lax.Precision.HIGHEST
    )
    return jnp.stack([real_part, imag_part], axis=-2)


def combine(earlier, latter):
    return complex_product(latter, earlier)


def shards(sections, launch_mode):
    regrouped = lax.all_to_all(sections, "wl", split_axis=1, concat_axis=4, tiled=True)
    forward_mats = regrouped[:, :, 0]
    backward_mats = regrouped[:, :, 1]
    modes = forward_mats.shape[-1]
    onehot = (jnp.arange(modes)[None, :] == launch_mode[:, None]).astype(jnp.float32) * math.sqrt(
        modes
    )
    launch_field = jnp.stack([onehot, jnp.zeros_like(onehot)], axis=1)

    def extend(running, matrix):
        nxt_mat = complex_product(matrix, running)
        return (nxt_mat, nxt_mat)

    last_forward, later_prefix = lax.scan(extend, forward_mats[0], forward_mats[1:])
    prefixes = jnp.concatenate([forward_mats[:1], later_prefix], axis=0)

    def shrink(running, matrix):
        return (complex_product(matrix, running), running)

    suffix_head, suffix_middle = lax.scan(
        shrink, backward_mats[-1], backward_mats[1:-1], reverse=True
    )
    suffixes = jnp.concatenate([suffix_head[None], suffix_middle], axis=0)
    backward_total = complex_product(backward_mats[0], suffix_head)
    unit_matrix = jnp.eye(modes, dtype=jnp.float32)
    identity_mats = jnp.broadcast_to(
        jnp.stack([unit_matrix, jnp.zeros_like(unit_matrix)], axis=0), last_forward.shape
    )
    forward_before = entering(last_forward, "sec", combine, identity_mats, False)
    backward_after = entering(backward_total, "sec", combine, identity_mats, True)
    entry_field = complex_apply(forward_before, launch_field)
    exit_field = complex_apply(backward_after, launch_field)
    forward_field = complex_apply(prefixes, entry_field)
    backward_field = jnp.concatenate(
        [complex_apply(suffixes, exit_field), exit_field[None]], axis=0
    )
    return (forward_field, backward_field)


def solution(mesh):
    return jax.shard_map(
        shards,
        mesh=mesh,
        in_specs=(P("sec", None, None, None, "wl", None), P("wl")),
        out_specs=(P("sec", "wl", None, None), P("sec", "wl", None, None)),
        check_vma=False,
    )
```

profile of v0, /device:TPU:454, one launch (start us, length us, event | category | flops | bytes accessed | tf_op | source)
XLA Modules:
  0.0 357.5 jit_solution(17075956038594746019)
XLA Ops:
  7.2 3.2 copy.14
  10.3 7.2 %all-to-all-start = ((f32[4,32,2,2,8,128]{5,4,3,2,0,1:T(8,128)}), f32[4,32,2,2,8,128]{5,4,3,2,0,1:T(8,128)S(1)}, u32[]{:S(2)}, u32[]{:S(2)}) async-start(f32[4,32,2,2,8,128]{5,4,3,2,0,1:T(8,128)} %copy.14), calls=%async_computation | async-start | bytes 4194304 | tf_op jit(solution)/shard_map/all_to_all | solution.py:56
  17.6 49.2 %all-to-all-done = f32[4,32,2,2,8,128]{5,4,3,2,0,1:T(8,128)S(1)} async-done(((f32[4,32,2,2,8,128]{5,4,3,2,0,1:T(8,128)}), f32[4,32,2,2,8,128]{5,4,3,2,0,1:T(8,128)S(1)}, u32[]{:S(2)}, u32[]{:S(2)}) %all-to-all-start) | async-done | bytes 2097184 | tf_op jit(solution)/shard_map/all_to_all | solution.py:56
  66.8 1.3 copy-done
  68.1 1.8 copy.75
  71.6 3.9 %while.52 = (s32[]{:T(128)}, f32[2,2,128,128]{3,2,0,1:T(8,128)S(1)}, f32[2,2,2,128,128]{4,3,1,2,0:T(8,128)}, f32[2,2,2,128,128]{4,3,1,2,0:T(8,128)S(1)}, s32[]{:T(128)}) while((s32[]{:T(128)}, f32[2,2,128,128]{3,2,0,1:T(8,128)S(1)}, f32[2,2,2,128,128]{4,3,1,2,0:T(8,128)}, f32[2,2,2,128,128]{4,3,1,2,0:T(8,128)S(1)}, s32[]{:T(128)}) %tuple.105), condition=%wide.region_5.6_spmd, body=%wide.region_4.5_spmd.sunk | while | flops 201457664 | bytes 7602313 | solution.py:75
  78.2 5.6 %while.50 = (s32[]{:T(128)}, f32[2,2,128,128]{3,2,0,1:T(8,128)S(1)}, f32[3,2,2,128,128]{4,3,1,2,0:T(8,128)}, f32[3,2,2,128,128]{4,3,1,2,0:T(8,128)S(1)}, s32[]{:T(128)}) while((s32[]{:T(128)}, f32[2,2,128,128]{3,2,0,1:T(8,128)S(1)}, f32[3,2,2,128,128]{4,3,1,2,0:T(8,128)}, f32[3,2,2,128,128]{4,3,1,2,0:T(8,128)S(1)}, s32[]{:T(128)}) %tuple.99), condition=%wide.region_1.2_spmd, body=%wide.region_0.1_spmd.sunk | while | flops 201457664 | bytes 3145805 | solution.py:69
  84.8 1.2 fusion.51
  86.0 88.7 %all-gather.7.cloned.1.call-done = f32[64,2,128,128]{2,3,0,1:T(8,128)} async-done(((f32[2,2,128,128]{2,3,0,1:T(8,128)}), f32[64,2,128,128]{2,3,0,1:T(8,128)}) %all-gather.7.cloned.1.call-update) | async-done | bytes 8388624 | tf_op jit(solution)/shard_map/all_gather | solution.py:13
  176.0 102.6 %all-gather.5.cloned.1.call-done = f32[64,2,128,128]{3,2,1,0:T(8,128)} async-done(((f32[2,2,128,128]{3,2,1,0:T(8,128)}), f32[64,2,128,128]{3,2,1,0:T(8,128)}) %all-gather.5.cloned.1.call-update) | async-done | bytes 8388624 | tf_op jit(solution)/shard_map/all_gather | solution.py:13
  278.6 65.7 %while.51 = (s32[]{:T(128)}, f32[2,2,128,128]{3,2,0,1:T(8,128)S(1)}, s32[]{:T(128)}, f32[32,2,2,128,128]{4,3,2,1,0:T(8,128)}, s32[]{:T(128)}, /*index=5*/s32[]{:T(128)}, s32[]{:T(128)}) while((s32[]{:T(128)}, f32[2,2,128,128]{3,2,0,1:T(8,128)S(1)}, s32[]{:T(128)}, f32[32,2,2,128,128]{4,3,2,1,0:T(8,128)}, s32[]{:T(128)}, /*index=5*/s32[]{:T(128)}, ...), condition=%wide.region_3.4_spmd, body=%wide.region_2.3_spmd.sunk | while | flops 201457664 | bytes 2883707 | solution.py:20
  278.7 1.0 copy_bitcast_fusion.3
  280.8 1.0 copy_bitcast_fusion.3
  282.9 1.0 copy_bitcast_fusion.3
  285.0 1.0 copy_bitcast_fusion.3
  287.2 1.0 copy_bitcast_fusion.3
  289.3 1.0 copy_bitcast_fusion.3
  291.4 1.0 copy_bitcast_fusion.3
  293.5 1.0 copy_bitcast_fusion.3
  295.6 1.0 copy_bitcast_fusion.3
  297.8 1.0 copy_bitcast_fusion.3
  299.9 1.0 copy_bitcast_fusion.3
  302.0 1.0 copy_bitcast_fusion.3
  304.1 1.0 copy_bitcast_fusion.3
  306.2 1.0 copy_bitcast_fusion.3
  308.4 1.0 copy_bitcast_fusion.3
  312.6 1.0 copy_bitcast_fusion.3
  314.7 1.0 copy_bitcast_fusion.3
  323.2 1.0 copy_bitcast_fusion.3
  333.8 1.0 copy_bitcast_fusion.3
  338.0 1.0 copy_bitcast_fusion.3
  340.2 1.0 copy_bitcast_fusion.3
  (262 shorter events, 65.5 us)
Async XLA Ops:
  10.3 56.4 %all-to-all-start = ((f32[4,32,2,2,8,128]{5,4,3,2,0,1:T(8,128)}), f32[4,32,2,2,8,128]{5,4,3,2,0,1:T(8,128)S(1)}, u32[]{:S(2)}, u32[]{:S(2)}) async-start(f32[4,32,2,2,8,128]{5,4,3,2,0,1:T(8,128)} %copy.14), calls=%async_computation | async-start | bytes 4194304 | tf_op jit(solution)/shard_map/all_to_all | solution.py:56
  17.5 157.1 %all-gather.7.cloned.1.call-start = ((), (), s32[]{:S(2)}) async-start(), calls=%async_computation.2 | async-start | bytes 8650752 | tf_op jit(solution)/shard_map/all_gather | solution.py:13
  66.8 1.3 copy-start
  71.6 1.1 copy-start.1
  72.8 0.8 copy-start.2
  73.6 1.1 copy-start.1
  74.8 0.8 copy-start.2
  78.0 200.6 %all-gather.5.cloned.1.call-start = ((), (), s32[]{:S(2)}) async-start(), calls=%async_computation.1 | async-start | bytes 8650752 | tf_op jit(solution)/shard_map/all_gather | solution.py:13
  78.2 6.4 %copy-start.5 = (s32[2]{0:T(128)S(1)}, s32[2]{0:T(128)}, u32[]{:S(2)}) copy-start(s32[2]{0:T(128)} %param.11) | copy-start | bytes 28
  78.2 6.5 %copy-start.3 = (f32[2,2,2,128,128]{4,3,1,2,0:T(8,128)S(1)}, f32[2,2,2,128,128]{4,3,1,2,0:T(8,128)}, u32[]{:S(2)}) copy-start(f32[2,2,2,128,128]{4,3,1,2,0:T(8,128)} %get-tuple-element.194) | copy-start | bytes 1572868
  83.8 1.0 copy-start.4
Sparse Core Ops, SparseCore 0:
  78.2 96.4 all-gather.6
  177.9 100.7 all-gather.4
where the time goes:
time: 359 us; the launch traced here: 358 us
  waiting for transfers between devices  240 us (67%)
  matrix products  46.8 us (13%)
  local copies, waits for them, and re-layouts  40.9 us (11%)
  between operations  14.2 us (4%)
  starting transfers between devices  7.29 us (2%)
  other arithmetic  5.63 us (2%)
    all_gather x2, waiting for transfers between devices, entering(): gathered = lax.all_gather(part, axis)  191 us
    all_to_all x1, waiting for transfers between devices, shards(): lax.all_to_all(sections, 'wl', split_axis=1, concat_axis=4, tiled=True)  49.2 us
    dot_general x148, matrix products, matrix_product(): return jnp.matmul(outer_mat, inner_mat, precision=lax.Precision.HIGHEST)  40 us
    squeeze x31, local copies, waits for them, and re-layouts, one(): return combine(state, lax.dynamic_index_in_dim(gathered, source, 0, False))  30.1 us
    all_to_all x1, starting transfers between devices, shards(): lax.all_to_all(sections, 'wl', split_axis=1, concat_axis=4, tiled=True)  7.21 us
  transfers between devices with their start and end apart: 3, of which 3 were waited for; matrix products, arithmetic and copies ran while one was open for 2% of the time, Pallas kernels for 0%

commit v1 on v0

v1 whole, which is shorter than its diff:
```python
import functools
import math

import jax
import jax.numpy as jnp
from jax import lax
from jax.experimental import pallas as pl
from jax.experimental.pallas import tpu as pltpu
from jax.sharding import Mesh, PartitionSpec as P

M = 128
F32 = jnp.float32
BF16 = jnp.bfloat16
VMEM_SPEC = pl.BlockSpec(memory_space=pltpu.VMEM)
SMEM_SPEC = pl.BlockSpec(memory_space=pltpu.SMEM)
HBM_SPEC = pl.BlockSpec(memory_space=pltpu.HBM)
PARAMS = pltpu.CompilerParams(vmem_limit_bytes=24 * 1024 * 1024)


def slot_of(zh, zl):
    return jnp.where(zh == 0, zl, 3 - zl)


def place():
    x, zh, zl = lax.axis_index("x"), lax.axis_index("zh"), lax.axis_index("zl")
    slot = slot_of(zh, zl)
    direction = lax.rem(slot, 2)
    spot = 2 * x + zh
    spot = jnp.where(direction == 0, spot, 7 - spot)
    return slot // 2, direction, lax.rem(spot, 4), spot // 4


def gather_kernel(sections, out, sem):
    zh = lax.axis_index("zh")
    copies = []
    for zl in range(4):
        slot = slot_of(zh, zl)
        for c in range(4):
            copy = pltpu.make_async_copy(sections.at[c, :, slot], out.at[:, zl, c], sem.at[zl, c])
            copy.start()
            copies.append(copy)
    for copy in copies:
        copy.wait()


def split(value):
    high = value.astype(BF16)
    return high, (value - high.astype(F32)).astype(BF16)


def as_left(mat):
    high, low = split(jnp.concatenate(mat, axis=1))
    return jnp.concatenate([high, low], axis=0), high


def as_right(mat):
    real, imag = mat
    real_high, real_low = split(real)
    imag_high, imag_low = split(imag)
    high = jnp.concatenate(
        [
            jnp.concatenate([real_high, imag_high], axis=1),
            jnp.concatenate([-imag_high, real_high], axis=1),
        ],
        axis=0,
    )
    low = jnp.concatenate(
        [
            jnp.concatenate([real_low, imag_low], axis=1),
            jnp.concatenate([-imag_low, real_low], axis=1),
        ],
        axis=0,
    )
    return high, low


def product(outer_mat, inner_mat):
    both, high = as_left(outer_mat)
    right_high, right_low = as_right(inner_mat)
    wide = jnp.dot(both, right_high, preferred_element_type=F32)
    more = jnp.dot(high, right_low, preferred_element_type=F32)
    total = wide[:M] + (wide[M:] + more)
    return total[:, :M], total[:, M:]


def section_of(recv, order, step):
    index = jnp.where(order == 0, step, 15 - step)
    zl, c = index // 4, lax.rem(index, 4)
    return tuple(recv[:, zl, c, part].reshape(M, M) for part in range(2))


def tree_kernel(recv, total, keep):
    _, direction, _, _ = place()
    level = [section_of(recv, direction, step) for step in range(16)]
    kept = 0
    while len(level) > 1:
        level = [product(level[2 * k + 1], level[2 * k]) for k in range(len(level) // 2)]
        if len(level) > 1:
            for k in range(0, len(level), 2):
                for part in range(2):
                    keep[kept, part] = level[k][part]
                kept += 1
    for part in range(2):
        total[part] = level[0][part]


def matvec(mat, vec, eye):
    mat_real, mat_imag = mat
    real, imag = vec
    out_real = jnp.sum(mat_real * real - mat_imag * imag, axis=1, keepdims=True)
    out_imag = jnp.sum(mat_real * imag + mat_imag * real, axis=1, keepdims=True)
    return (
        jnp.sum(jnp.where(eye, out_real, 0.0), axis=0, keepdims=True),
        jnp.sum(jnp.where(eye, out_imag, 0.0), axis=0, keepdims=True),
    )


def diagonal():
    return lax.broadcasted_iota(jnp.int32, (M, M), 0) == lax.broadcasted_iota(jnp.int32, (M, M), 1)


def launch_vector(mode, b):
    lane = lax.broadcasted_iota(jnp.int32, (1, M), 1)
    onehot = jnp.where(lane == mode[b], jnp.float32(math.sqrt(M)), 0.0)
    return onehot, jnp.zeros_like(onehot)


def middle_kernel(mode, own, near, beside, across, middle, mats):
    b, _, spot, _ = place()
    for s, ref in enumerate((own, near, beside, across)):
        mats[s] = ref[...]
    eye = diagonal()
    vec = launch_vector(mode, b)
    for step in range(4):
        which = spot ^ step
        vec = matvec((mats[which, 0], mats[which, 1]), vec, eye)
    middle[0:1] = vec[0]
    middle[1:2] = vec[1]
    middle[2:8] = jnp.zeros((6, M), F32)


def fields_kernel(mode, own, near, beside, across, middle, recv, keep, out, mats):
    b, direction, spot, upper = place()
    for s, ref in enumerate((own, near, beside, across)):
        mats[s] = ref[...]
    eye = diagonal()
    launch = launch_vector(mode, b)
    start = tuple(jnp.where(upper == 1, middle[part : part + 1], launch[part]) for part in range(2))

    def enter(step, vec):
        which = spot ^ step
        return matvec((mats[which, 0], mats[which, 1]), vec, eye)

    states = [None] * 17
    states[0] = lax.fori_loop(0, spot, enter, start)

    def kept(k):
        return keep[k, 0], keep[k, 1]

    states[16] = matvec((own[0], own[1]), states[0], eye)
    states[8] = matvec(kept(6), states[0], eye)
    for k in range(2):
        states[8 * k + 4] = matvec(kept(4 + k), states[8 * k], eye)
    for k in range(4):
        states[4 * k + 2] = matvec(kept(k), states[4 * k], eye)
    for k in range(8):
        states[2 * k + 1] = matvec(section_of(recv, direction, 2 * k), states[2 * k], eye)
    for index in range(16):
        for part in range(2):
            out[index // 4, 2 * (index % 4) + part : 2 * (index % 4) + part + 1] = jnp.where(
                direction == 0, states[index + 1][part], states[15 - index][part]
            )


def output_kernel(returned, forward, backward):
    zh = lax.axis_index("zh")
    for b in range(2):
        for d, ref in enumerate((forward, backward)):
            block = returned[slot_of(zh, 2 * b + d)]
            for c in range(4):
                ref[c, b] = block[2 * c : 2 * c + 2]


def shards(sections, launch_mode):
    sections = sections.reshape(4, 16, 4, 2, 8, M)
    send = pl.pallas_call(
        gather_kernel,
        out_shape=jax.ShapeDtypeStruct((16, 4, 4, 2, 8, M), F32),
        in_specs=[HBM_SPEC],
        out_specs=VMEM_SPEC,
        scratch_shapes=[pltpu.SemaphoreType.DMA((4, 4))],
        compiler_params=PARAMS,
        name="gather",
    )(sections)
    recv = lax.all_to_all(send.reshape(64, 4, 2, 8, M), ("y", "core", "zl"), 0, 0)
    recv = recv.reshape(16, 4, 4, 2, 8, M)
    total, keep = pl.pallas_call(
        tree_kernel,
        out_shape=(
            jax.ShapeDtypeStruct((2, M, M), F32),
            jax.ShapeDtypeStruct((7, 2, M, M), F32),
        ),
        in_specs=[VMEM_SPEC],
        out_specs=(VMEM_SPEC, VMEM_SPEC),
        compiler_params=PARAMS,
        name="tree",
    )(recv)
    turn = [(x, x ^ 1) for x in range(4)]
    flip = [(z, 7 - z) for z in range(8)]
    both = [(8 * x + z, 8 * (x ^ 1) + 7 - z) for x in range(4) for z in range(8)]
    near = lax.ppermute(total, ("zh", "zl"), flip)
    beside = lax.ppermute(total, "x", turn)
    across = lax.ppermute(total, ("x", "zh", "zl"), both)
    middle = pl.pallas_call(
        middle_kernel,
        out_shape=jax.ShapeDtypeStruct((8, M), F32),
        in_specs=[SMEM_SPEC] + [VMEM_SPEC] * 4,
        out_specs=VMEM_SPEC,
        scratch_shapes=[pltpu.VMEM((4, 2, M, M), F32)],
        compiler_params=PARAMS,
        name="middle",
    )(launch_mode, total, near, beside, across)
    middle = lax.ppermute(middle, "x", [(x, x ^ 2) for x in range(4)])
    fields = pl.pallas_call(
        fields_kernel,
        out_shape=jax.ShapeDtypeStruct((4, 8, M), F32),
        in_specs=[SMEM_SPEC] + [VMEM_SPEC] * 7,
        out_specs=VMEM_SPEC,
        scratch_shapes=[pltpu.VMEM((4, 2, M, M), F32)],
        compiler_params=PARAMS,
        name="fields",
    )(launch_mode, total, near, beside, across, middle, recv, keep)
    returned = lax.all_to_all(fields, "zl", 0, 0)
    return pl.pallas_call(
        output_kernel,
        out_shape=(
            jax.ShapeDtypeStruct((4, 2, 2, M), F32),
            jax.ShapeDtypeStruct((4, 2, 2, M), F32),
        ),
        in_specs=[VMEM_SPEC],
        out_specs=(VMEM_SPEC, VMEM_SPEC),
        compiler_params=PARAMS,
        name="outputs",
    )(returned)


def solution(mesh):
    fine = Mesh(mesh.devices.reshape(8, 2, 4, 2, 4), ("y", "core", "x", "zh", "zl"))
    return jax.shard_map(
        shards,
        mesh=fine,
        in_specs=(P(("x", "zh", "zl"), None, None, None, ("y", "core"), None), P(("y", "core"))),
        out_specs=(
            P(("x", "zh", "zl"), ("y", "core"), None, None),
            P(("x", "zh", "zl"), ("y", "core"), None, None),
        ),
        check_vma=False,
    )
```

time: 359 us -> 109 us (0.30)
  the two profiles are of different devices: /device:TPU:454 before, /device:TPU:2 now
where the time goes in v1:
time: 109 us; the launch traced here: 108 us
  blocking collectives  73 us (67%)
  starting transfers between devices  17.6 us (16%)
  waiting for transfers between devices  10.7 us (10%)
  Pallas kernels  4.87 us (4%)
  local copies, waits for them, and re-layouts  1.59 us (1%)
    all_to_all x1, blocking collectives, shards(): lax.all_to_all(send.reshape(64, 4, 2, 8, M), ('y', 'core', 'zl'), 0, 0)  64.7 us
    all_to_all x1, blocking collectives, shards(): returned = lax.all_to_all(fields, 'zl', 0, 0)  8.3 us
    ppermute x1, starting transfers between devices, shards(): across = lax.ppermute(total, ('x', 'zh', 'zl'), both)  8.22 us
    ppermute x1, waiting for transfers between devices, shards(): near = lax.ppermute(total, ('zh', 'zl'), flip)  5.39 us
    ppermute x1, starting transfers between devices, shards(): middle = lax.ppermute(middle, 'x', [(x, x ^ 2) for x in range(4)])  4.03 us
    ppermute x1, starting transfers between devices, shards(): beside = lax.ppermute(total, 'x', turn)  3.39 us
    ppermute x1, waiting for transfers between devices, shards(): middle = lax.ppermute(middle, 'x', [(x, x ^ 2) for x in range(4)])  2.96 us
    ppermute x1, waiting for transfers between devices, shards(): beside = lax.ppermute(total, 'x', turn)  2.38 us
  transfers between devices with their start and end apart: 4, of which 3 were waited for; matrix products, arithmetic and copies ran while one was open for 0% of the time, Pallas kernels for 0%

profile of v1, /device:TPU:2, one launch (start us, length us, event | category | flops | bytes accessed | tf_op | source)
XLA Modules:
  0.0 108.5 jit_solution(11656918492266889840)
XLA Ops:
  0.6 0.0 copy-start
  0.6 1.6 %copy-done = f32[4,32,2,2,8,128]{5,4,3,2,1,0:T(8,128)S(1)} copy-done((f32[4,32,2,2,8,128]{5,4,3,2,1,0:T(8,128)S(1)}, f32[4,32,2,2,8,128]{5,4,3,2,1,0:T(8,128)}, u32[]{:S(2)}) %copy-start) | copy-done | bytes 2097176
  2.2 0.5 gather.1
  2.7 64.7 %all_to_all.10 = f32[64,4,2,8,128]{4,3,2,1,0:T(8,128)S(1)} all-to-all(f32[64,4,2,8,128]{4,3,2,1,0:T(8,128)S(1)} %bitcast.5), channel_id=1, replica_groups=mesh['y'=8,'core'=2,'x'=4,'zh'=2,'zl'=4] {'y','core','zl'}, dimensions={0} | all-to-all | bytes 4194304 | tf_op jit(solution)/shard_map/all_to_all | solution.py:195
  67.4 0.0 copy-start.1
  67.4 1.2 %tree.1 = (f32[2,128,128]{2,1,0:T(8,128)S(1)}, f32[7,2,128,128]{3,2,1,0:T(8,128)S(1)}) custom-call(f32[16,4,4,2,8,128]{5,4,3,2,1,0:T(8,128)S(1)} %bitcast.3), custom_call_target="tpu_custom_call" | custom-call | tf_op jit(solution)/shard_map/tree/pallas_call | solution.py:197
  68.7 8.2 %collective-permute-start.2 = (f32[2,128,128]{2,1,0:T(8,128)S(1)}, f32[2,128,128]{2,1,0:T(8,128)S(1)}, u32[]{:S(2)}, u32[]{:S(2)}) collective-permute-start(f32[2,128,128]{2,1,0:T(8,128)S(1)} %get-tuple-element.4.own), channel_id=1, source_target_pairs={{0,15},{1,14},{2,13},{3,12},{4,11},{5,10},{6,9},{7,8},{8,7},{9,6},... | collective-permute-start | bytes 393224 | tf_op jit(solution)/shard_map/ppermute | solution.py:213
  76.9 3.4 %collective-permute-start.1 = (f32[2,128,128]{2,1,0:T(8,128)S(1)}, f32[2,128,128]{2,1,0:T(8,128)S(1)}, u32[]{:S(2)}, u32[]{:S(2)}) collective-permute-start(f32[2,128,128]{2,1,0:T(8,128)S(1)} %get-tuple-element.4.own), channel_id=1, source_target_pairs={{0,8},{8,0},{16,24},{24,16},{1,9},{9,1},{17,25},{25,17},{2,10},{10... | collective-permute-start | bytes 393224 | tf_op jit(solution)/shard_map/ppermute | solution.py:212
  80.3 1.9 %collective-permute-start = (f32[2,128,128]{2,1,0:T(8,128)S(1)}, f32[2,128,128]{2,1,0:T(8,128)S(1)}, u32[]{:S(2)}, u32[]{:S(2)}) collective-permute-start(f32[2,128,128]{2,1,0:T(8,128)S(1)} %get-tuple-element.4.own), channel_id=1, source_target_pairs={{0,7},{1,6},{2,5},{3,4},{4,3},{5,2},{6,1},{7,0},{8,15},{9,14},{10,... | collective-permute-start | bytes 393224 | tf_op jit(solution)/shard_map/ppermute | solution.py:211
  82.2 0.0 collective-permute-done.2.across
  82.2 2.4 %collective-permute-done.1.beside = f32[2,128,128]{2,1,0:T(8,128)S(1)} collective-permute-done((f32[2,128,128]{2,1,0:T(8,128)S(1)}, f32[2,128,128]{2,1,0:T(8,128)S(1)}, u32[]{:S(2)}, u32[]{:S(2)}) %collective-permute-start.1) | collective-permute-done | bytes 131104 | tf_op jit(solution)/shard_map/ppermute | solution.py:212
  84.6 5.4 %collective-permute-done.near = f32[2,128,128]{2,1,0:T(8,128)S(1)} collective-permute-done((f32[2,128,128]{2,1,0:T(8,128)S(1)}, f32[2,128,128]{2,1,0:T(8,128)S(1)}, u32[]{:S(2)}, u32[]{:S(2)}) %collective-permute-start) | collective-permute-done | bytes 131104 | tf_op jit(solution)/shard_map/ppermute | solution.py:211
  90.0 0.0 copy-done.1
  90.0 1.0 middle.1
  91.0 4.0 %collective-permute-start.3 = (f32[8,128]{1,0:T(8,128)S(1)}, f32[8,128]{1,0:T(8,128)S(1)}, u32[]{:S(2)}, u32[]{:S(2)}) collective-permute-start(f32[8,128]{1,0:T(8,128)S(1)} %middle.1), channel_id=1, source_target_pairs={{0,16},{8,24},{16,0},{24,8},{1,17},{9,25},{17,1},{25,9},{2,18},{10... | collective-permute-start | bytes 12296 | tf_op jit(solution)/shard_map/ppermute | solution.py:223
  95.1 3.0 %collective-permute-done.3.middle = f32[8,128]{1,0:T(8,128)S(1)} collective-permute-done((f32[8,128]{1,0:T(8,128)S(1)}, f32[8,128]{1,0:T(8,128)S(1)}, u32[]{:S(2)}, u32[]{:S(2)}) %collective-permute-start.3) | collective-permute-done | bytes 4128 | tf_op jit(solution)/shard_map/ppermute | solution.py:223
  98.0 1.5 %fields.1 = f32[4,8,128]{2,1,0:T(8,128)S(1)} custom-call(s32[2]{0:T(128)S(1)} %copy-done.1, f32[2,128,128]{2,1,0:T(8,128)S(1)} %get-tuple-element.4.own, f32[2,128,128]{2,1,0:T(8,128)S(1)} %collective-permute-done.near, f32[2,128,128]{2,1,0:T(8,128)S(1)} %collective-permute-done.1.beside, f32[2,128,128]{2,1,0:T(8,128)S(1)} %collective-permute-done.2.across, ...), custom_call_target="tpu_custom_call" | custom-call | tf_op jit(solution)/shard_map/fields/pallas_call | solution.py:224
  99.6 8.3 %all_to_all.11.returned = f32[4,8,128]{2,1,0:T(8,128)S(1)} all-to-all(f32[4,8,128]{2,1,0:T(8,128)S(1)} %fields.1), channel_id=1, replica_groups=mesh['y'=8,'core'=2,'x'=4,'zh'=2,'zl'=4] {'zl'}, dimensions={0} | all-to-all | bytes 32768 | tf_op jit(solution)/shard_map/all_to_all | solution.py:233
  107.9 0.6 outputs.1
Async XLA Ops:
  0.6 1.6 %copy-start = (f32[4,32,2,2,8,128]{5,4,3,2,1,0:T(8,128)S(1)}, f32[4,32,2,2,8,128]{5,4,3,2,1,0:T(8,128)}, u32[]{:S(2)}) copy-start(f32[4,32,2,2,8,128]{5,4,3,2,1,0:T(8,128)} %param.2) | copy-start | bytes 6291460
  67.4 22.6 %copy-start.1 = (s32[2]{0:T(128)S(1)}, s32[2]{0:T(128)}, u32[]{:S(2)}) copy-start(s32[2]{0:T(128)} %mode.3) | copy-start | bytes 28
  68.7 13.6 %collective-permute-start.2 = (f32[2,128,128]{2,1,0:T(8,128)S(1)}, f32[2,128,128]{2,1,0:T(8,128)S(1)}, u32[]{:S(2)}, u32[]{:S(2)}) collective-permute-start(f32[2,128,128]{2,1,0:T(8,128)S(1)} %get-tuple-element.4.own), channel_id=1, source_target_pairs={{0,15},{1,14},{2,13},{3,12},{4,11},{5,10},{6,9},{7,8},{8,7},{9,6},... | collective-permute-start | bytes 393224 | tf_op jit(solution)/shard_map/ppermute | solution.py:213
  76.9 7.7 %collective-permute-start.1 = (f32[2,128,128]{2,1,0:T(8,128)S(1)}, f32[2,128,128]{2,1,0:T(8,128)S(1)}, u32[]{:S(2)}, u32[]{:S(2)}) collective-permute-start(f32[2,128,128]{2,1,0:T(8,128)S(1)} %get-tuple-element.4.own), channel_id=1, source_target_pairs={{0,8},{8,0},{16,24},{24,16},{1,9},{9,1},{17,25},{25,17},{2,10},{10... | collective-permute-start | bytes 393224 | tf_op jit(solution)/shard_map/ppermute | solution.py:212
  80.3 9.7 %collective-permute-start = (f32[2,128,128]{2,1,0:T(8,128)S(1)}, f32[2,128,128]{2,1,0:T(8,128)S(1)}, u32[]{:S(2)}, u32[]{:S(2)}) collective-permute-start(f32[2,128,128]{2,1,0:T(8,128)S(1)} %get-tuple-element.4.own), channel_id=1, source_target_pairs={{0,7},{1,6},{2,5},{3,4},{4,3},{5,2},{6,1},{7,0},{8,15},{9,14},{10,... | collective-permute-start | bytes 393224 | tf_op jit(solution)/shard_map/ppermute | solution.py:211
  91.0 7.0 %collective-permute-start.3 = (f32[8,128]{1,0:T(8,128)S(1)}, f32[8,128]{1,0:T(8,128)S(1)}, u32[]{:S(2)}, u32[]{:S(2)}) collective-permute-start(f32[8,128]{1,0:T(8,128)S(1)} %middle.1), channel_id=1, source_target_pairs={{0,16},{8,24},{16,0},{24,8},{1,17},{9,25},{17,1},{25,9},{2,18},{10... | collective-permute-start | bytes 12296 | tf_op jit(solution)/shard_map/ppermute | solution.py:223

commit v2 on v1

--- a/solution.py
+++ b/solution.py
@@ -30,13 +30,25 @@
     return slot // 2, direction, lax.rem(spot, 4), spot // 4
 
 
-def gather_kernel(sections, out, sem):
+def gather_kernel(sections, out, stage, read_sem, sem):
     zh = lax.axis_index("zh")
+    reads = []
+    for c in range(4):
+        for part in range(4):
+            rows = pl.ds(4 * part, 4)
+            read = pltpu.make_async_copy(
+                sections.at[c, rows], stage.at[c, rows], read_sem.at[c, part]
+            )
+            read.start()
+            reads.append(read)
     copies = []
-    for zl in range(4):
-        slot = slot_of(zh, zl)
-        for c in range(4):
-            copy = pltpu.make_async_copy(sections.at[c, :, slot], out.at[:, zl, c], sem.at[zl, c])
+    for c in range(4):
+        for read in reads[4 * c : 4 * c + 4]:
+            read.wait()
+        for zl in range(4):
+            copy = pltpu.make_async_copy(
+                stage.at[c, :, slot_of(zh, zl)], out.at[:, zl, c], sem.at[zl, c]
+            )
             copy.start()
             copies.append(copy)
     for copy in copies:
@@ -125,34 +137,33 @@
     return onehot, jnp.zeros_like(onehot)
 
 
-def middle_kernel(mode, own, near, beside, across, middle, mats):
-    b, _, spot, _ = place()
-    for s, ref in enumerate((own, near, beside, across)):
-        mats[s] = ref[...]
+def pair_kernel(own, near, pair):
+    _, _, spot, _ = place()
+    odd = lax.rem(spot, 2) == 1
+    first = tuple(jnp.where(odd, near[part], own[part]) for part in range(2))
+    second = tuple(jnp.where(odd, own[part], near[part]) for part in range(2))
+    result = product(second, first)
+    for part in range(2):
+        for s in range(4):
+            pair[s, part] = result[part]
+
+
+def fields_kernel(mode, own, near, mats, recv, keep, out):
+    b, direction, spot, upper = place()
+    column = 2 * upper + spot // 2
     eye = diagonal()
-    vec = launch_vector(mode, b)
-    for step in range(4):
-        which = spot ^ step
-        vec = matvec((mats[which, 0], mats[which, 1]), vec, eye)
-    middle[0:1] = vec[0]
-    middle[1:2] = vec[1]
-    middle[2:8] = jnp.zeros((6, M), F32)
-
-
-def fields_kernel(mode, own, near, beside, across, middle, recv, keep, out, mats):
-    b, direction, spot, upper = place()
-    for s, ref in enumerate((own, near, beside, across)):
-        mats[s] = ref[...]
-    eye = diagonal()
-    launch = launch_vector(mode, b)
-    start = tuple(jnp.where(upper == 1, middle[part : part + 1], launch[part]) for part in range(2))
 
     def enter(step, vec):
-        which = spot ^ step
+        which = jnp.where(direction == 0, step, 3 - step)
         return matvec((mats[which, 0], mats[which, 1]), vec, eye)
 
+    vec = lax.fori_loop(0, column, enter, launch_vector(mode, b))
+
+    def step_in(step, vec):
+        return matvec((near[0], near[1]), vec, eye)
+
     states = [None] * 17
-    states[0] = lax.fori_loop(0, spot, enter, start)
+    states[0] = lax.fori_loop(0, lax.rem(spot, 2), step_in, vec)
 
     def kept(k):
         return keep[k, 0], keep[k, 1]
@@ -188,8 +199,12 @@
         out_shape=jax.ShapeDtypeStruct((16, 4, 4, 2, 8, M), F32),
         in_specs=[HBM_SPEC],
         out_specs=VMEM_SPEC,
-        scratch_shapes=[pltpu.SemaphoreType.DMA((4, 4))],
-        compiler_params=PARAMS,
+        scratch_shapes=[
+            pltpu.VMEM((4, 16, 4, 2, 8, M), F32),
+            pltpu.SemaphoreType.DMA((4, 4)),
+            pltpu.SemaphoreType.DMA((4, 4)),
+        ],
+        compiler_params=pltpu.CompilerParams(vmem_limit_bytes=60 * 1024 * 1024),
         name="gather",
     )(sections)
     recv = lax.all_to_all(send.reshape(64, 4, 2, 8, M), ("y", "core", "zl"), 0, 0)
@@ -205,31 +220,24 @@
         compiler_params=PARAMS,
         name="tree",
     )(recv)
-    turn = [(x, x ^ 1) for x in range(4)]
-    flip = [(z, 7 - z) for z in range(8)]
-    both = [(8 * x + z, 8 * (x ^ 1) + 7 - z) for x in range(4) for z in range(8)]
-    near = lax.ppermute(total, ("zh", "zl"), flip)
-    beside = lax.ppermute(total, "x", turn)
-    across = lax.ppermute(total, ("x", "zh", "zl"), both)
-    middle = pl.pallas_call(
-        middle_kernel,
-        out_shape=jax.ShapeDtypeStruct((8, M), F32),
-        in_specs=[SMEM_SPEC] + [VMEM_SPEC] * 4,
+    near = lax.ppermute(total, ("zh", "zl"), [(z, 7 - z) for z in range(8)])
+    pair = pl.pallas_call(
+        pair_kernel,
+        out_shape=jax.ShapeDtypeStruct((4, 2, M, M), F32),
+        in_specs=[VMEM_SPEC] * 2,
         out_specs=VMEM_SPEC,
-        scratch_shapes=[pltpu.VMEM((4, 2, M, M), F32)],
-        compiler_params=PARAMS,
-        name="middle",
-    )(launch_mode, total, near, beside, across)
-    middle = lax.ppermute(middle, "x", [(x, x ^ 2) for x in range(4)])
+        compiler_params=PARAMS,
+        name="pair",
+    )(total, near)
+    mats = lax.all_to_all(pair, "x", 0, 0)
     fields = pl.pallas_call(
         fields_kernel,
         out_shape=jax.ShapeDtypeStruct((4, 8, M), F32),
-        in_specs=[SMEM_SPEC] + [VMEM_SPEC] * 7,
+        in_specs=[SMEM_SPEC] + [VMEM_SPEC] * 5,
         out_specs=VMEM_SPEC,
-        scratch_shapes=[pltpu.VMEM((4, 2, M, M), F32)],
         compiler_params=PARAMS,
         name="fields",
-    )(launch_mode, total, near, beside, across, middle, recv, keep)
+    )(launch_mode, total, near, mats, recv, keep)
     returned = lax.all_to_all(fields, "zl", 0, 0)
     return pl.pallas_call(
         output_kernel,

time: 109 us -> 107 us (0.982)
  the two profiles are of different devices: /device:TPU:2 before, /device:TPU:8 now
where the time goes in v2:
time: 107 us
  blocking collectives  84.5 us (79%)
  starting transfers between devices  8.9 us (8%)
  Pallas kernels  6.7 us (6%)
  waiting for transfers between devices  5.92 us (6%)
    all_to_all x1, blocking collectives, shards(): lax.all_to_all(send.reshape(64, 4, 2, 8, M), ('y', 'core', 'zl'), 0, 0)  63.3 us
    all_to_all x1, blocking collectives, shards(): mats = lax.all_to_all(pair, 'x', 0, 0)  13.3 us
    ppermute x1, starting transfers between devices, shards(): near = lax.ppermute(total, ('zh', 'zl'), [(z, 7 - z) for z in range(8)])  8.9 us
    all_to_all x1, blocking collectives, shards(): returned = lax.all_to_all(fields, 'zl', 0, 0)  7.96 us
    ppermute x1, waiting for transfers between devices, shards(): near = lax.ppermute(total, ('zh', 'zl'), [(z, 7 - z) for z in range(8)])  5.92 us
    pallas_call x1, Pallas kernels, shards(): pl.pallas_call(gather_kernel, out_shape=jax.ShapeDtypeStruct((16, 4, 4, 2...  3.32 us
  transfers between devices with their start and end apart: 1, of which 1 were waited for; matrix products, arithmetic and copies ran while one was open for 0% of the time, Pallas kernels for 0%

profile of v2, /device:TPU:8, one launch (start us, length us, event | category | flops | bytes accessed | tf_op | source)
XLA Modules:
  0.0 106.7 jit_solution(8588906154588107348)
XLA Ops:
  0.6 3.3 %gather.1 = f32[16,4,4,2,8,128]{5,4,3,2,1,0:T(8,128)} custom-call(f32[4,16,4,2,8,128]{5,4,3,2,1,0:T(8,128)} %bitcast.6), custom_call_target="tpu_custom_call" | custom-call | tf_op jit(solution)/shard_map/gather/pallas_call | solution.py:197
  4.0 63.3 %all_to_all.15 = f32[64,4,2,8,128]{4,3,2,1,0:T(8,128)S(1)} all-to-all(f32[64,4,2,8,128]{4,3,2,1,0:T(8,128)} %bitcast.5), channel_id=1, replica_groups=mesh['y'=8,'core'=2,'x'=4,'zh'=2,'zl'=4] {'y','core','zl'}, dimensions={0} | all-to-all | bytes 4194304 | tf_op jit(solution)/shard_map/all_to_all | solution.py:210
  67.2 0.0 copy-start
  67.2 1.3 %tree.1 = (f32[2,128,128]{2,1,0:T(8,128)S(1)}, f32[7,2,128,128]{3,2,1,0:T(8,128)S(1)}) custom-call(f32[16,4,4,2,8,128]{5,4,3,2,1,0:T(8,128)S(1)} %bitcast.3), custom_call_target="tpu_custom_call" | custom-call | tf_op jit(solution)/shard_map/tree/pallas_call | solution.py:212
  68.5 8.9 %collective-permute-start = (f32[2,128,128]{2,1,0:T(8,128)S(1)}, f32[2,128,128]{2,1,0:T(8,128)S(1)}, u32[]{:S(2)}, u32[]{:S(2)}) collective-permute-start(f32[2,128,128]{2,1,0:T(8,128)S(1)} %get-tuple-element.4.own), channel_id=1, source_target_pairs={{0,7},{1,6},{2,5},{3,4},{4,3},{5,2},{6,1},{7,0},{8,15},{9,14},{10,... | collective-permute-start | bytes 393224 | tf_op jit(solution)/shard_map/ppermute | solution.py:223
  77.4 5.9 %collective-permute-done.near = f32[2,128,128]{2,1,0:T(8,128)S(1)} collective-permute-done((f32[2,128,128]{2,1,0:T(8,128)S(1)}, f32[2,128,128]{2,1,0:T(8,128)S(1)}, u32[]{:S(2)}, u32[]{:S(2)}) %collective-permute-start) | collective-permute-done | bytes 131104 | tf_op jit(solution)/shard_map/ppermute | solution.py:223
  83.3 0.2 pair.1
  83.6 13.3 %all_to_all.16.mats = f32[4,2,128,128]{3,2,1,0:T(8,128)S(1)} all-to-all(f32[4,2,128,128]{3,2,1,0:T(8,128)S(1)} %pair.1), channel_id=1, replica_groups=mesh['y'=8,'core'=2,'x'=4,'zh'=2,'zl'=4] {'x'}, dimensions={0} | all-to-all | bytes 1048576 | tf_op jit(solution)/shard_map/all_to_all | solution.py:232
  96.9 0.0 copy-done
  96.9 1.3 %fields.1 = f32[4,8,128]{2,1,0:T(8,128)S(1)} custom-call(s32[2]{0:T(128)S(1)} %copy-done, f32[2,128,128]{2,1,0:T(8,128)S(1)} %get-tuple-element.4.own, f32[2,128,128]{2,1,0:T(8,128)S(1)} %collective-permute-done.near, f32[4,2,128,128]{3,2,1,0:T(8,128)S(1)} %all_to_all.16.mats, f32[16,4,4,2,8,128]{5,4,3,2,1,0:T(8,128)S(1)} %bitcast.4, ...), custom_call_target="tpu_custom_call" | custom-call | tf_op jit(solution)/shard_map/fields/pallas_call | solution.py:233
  98.1 8.0 %all_to_all.17.returned = f32[4,8,128]{2,1,0:T(8,128)S(1)} all-to-all(f32[4,8,128]{2,1,0:T(8,128)S(1)} %fields.1), channel_id=1, replica_groups=mesh['y'=8,'core'=2,'x'=4,'zh'=2,'zl'=4] {'zl'}, dimensions={0} | all-to-all | bytes 32768 | tf_op jit(solution)/shard_map/all_to_all | solution.py:241
  106.1 0.6 outputs.1
Async XLA Ops:
  67.2 29.6 %copy-start = (s32[2]{0:T(128)S(1)}, s32[2]{0:T(128)}, u32[]{:S(2)}) copy-start(s32[2]{0:T(128)} %mode.1) | copy-start | bytes 28
  68.5 14.8 %collective-permute-start = (f32[2,128,128]{2,1,0:T(8,128)S(1)}, f32[2,128,128]{2,1,0:T(8,128)S(1)}, u32[]{:S(2)}, u32[]{:S(2)}) collective-permute-start(f32[2,128,128]{2,1,0:T(8,128)S(1)} %get-tuple-element.4.own), channel_id=1, source_target_pairs={{0,7},{1,6},{2,5},{3,4},{4,3},{5,2},{6,1},{7,0},{8,15},{9,14},{10,... | collective-permute-start | bytes 393224 | tf_op jit(solution)/shard_map/ppermute | solution.py:223

commit v3 on v2

--- a/solution.py
+++ b/solution.py
@@ -1,4 +1,3 @@
-import functools
 import math
 
 import jax
@@ -30,25 +29,13 @@
     return slot // 2, direction, lax.rem(spot, 4), spot // 4
 
 
-def gather_kernel(sections, out, stage, read_sem, sem):
+def gather_kernel(sections, out, sem):
     zh = lax.axis_index("zh")
-    reads = []
-    for c in range(4):
-        for part in range(4):
-            rows = pl.ds(4 * part, 4)
-            read = pltpu.make_async_copy(
-                sections.at[c, rows], stage.at[c, rows], read_sem.at[c, part]
-            )
-            read.start()
-            reads.append(read)
     copies = []
-    for c in range(4):
-        for read in reads[4 * c : 4 * c + 4]:
-            read.wait()
-        for zl in range(4):
-            copy = pltpu.make_async_copy(
-                stage.at[c, :, slot_of(zh, zl)], out.at[:, zl, c], sem.at[zl, c]
-            )
+    for zl in range(4):
+        slot = slot_of(zh, zl)
+        for c in range(4):
+            copy = pltpu.make_async_copy(sections.at[c, :, slot], out.at[:, zl, c], sem.at[zl, c])
             copy.start()
             copies.append(copy)
     for copy in copies:
@@ -137,7 +124,29 @@
     return onehot, jnp.zeros_like(onehot)
 
 
-def pair_kernel(own, near, pair):
+def prefix_kernel(recv, keep, total, turned):
+    _, direction, _, _ = place()
+
+    def kept(k):
+        return keep[k, 0], keep[k, 1]
+
+    def section(step):
+        return section_of(recv, direction, step)
+
+    prefix = {1: section(0), 2: kept(0), 4: kept(4), 8: kept(6), 16: (total[0], total[1])}
+    prefix[6] = product(kept(1), prefix[4])
+    prefix[10] = product(kept(2), prefix[8])
+    prefix[12] = product(kept(5), prefix[8])
+    prefix[14] = product(kept(3), prefix[12])
+    for step in range(2, 16, 2):
+        prefix[step + 1] = product(section(step), prefix[step])
+    for step in range(1, 17):
+        for part in range(2):
+            turned[step - 1, part] = prefix[step][part].T
+
+
+def pair_kernel(own, near, turned, pair):
+    del turned
     _, _, spot, _ = place()
     odd = lax.rem(spot, 2) == 1
     first = tuple(jnp.where(odd, near[part], own[part]) for part in range(2))
@@ -148,7 +157,7 @@
             pair[s, part] = result[part]
 
 
-def fields_kernel(mode, own, near, mats, recv, keep, out):
+def fields_kernel(mode, near, mats, turned, out):
     b, direction, spot, upper = place()
     column = 2 * upper + spot // 2
     eye = diagonal()
@@ -162,20 +171,19 @@
     def step_in(step, vec):
         return matvec((near[0], near[1]), vec, eye)
 
-    states = [None] * 17
-    states[0] = lax.fori_loop(0, lax.rem(spot, 2), step_in, vec)
-
-    def kept(k):
-        return keep[k, 0], keep[k, 1]
-
-    states[16] = matvec((own[0], own[1]), states[0], eye)
-    states[8] = matvec(kept(6), states[0], eye)
-    for k in range(2):
-        states[8 * k + 4] = matvec(kept(4 + k), states[8 * k], eye)
-    for k in range(4):
-        states[4 * k + 2] = matvec(kept(k), states[4 * k], eye)
-    for k in range(8):
-        states[2 * k + 1] = matvec(section_of(recv, direction, 2 * k), states[2 * k], eye)
+    entering = lax.fori_loop(0, lax.rem(spot, 2), step_in, vec)
+    real, imag = (
+        jnp.sum(jnp.where(eye, entering[part], 0.0), axis=1, keepdims=True) for part in range(2)
+    )
+    states = [entering]
+    for step in range(16):
+        mat_real, mat_imag = turned[step, 0], turned[step, 1]
+        states.append(
+            (
+                jnp.sum(mat_real * real - mat_imag * imag, axis=0, keepdims=True),
+                jnp.sum(mat_real * imag + mat_imag * real, axis=0, keepdims=True),
+            )
+        )
     for index in range(16):
         for part in range(2):
             out[index // 4, 2 * (index % 4) + part : 2 * (index % 4) + part + 1] = jnp.where(
@@ -199,12 +207,8 @@
         out_shape=jax.ShapeDtypeStruct((16, 4, 4, 2, 8, M), F32),
         in_specs=[HBM_SPEC],
         out_specs=VMEM_SPEC,
-        scratch_shapes=[
-            pltpu.VMEM((4, 16, 4, 2, 8, M), F32),
-            pltpu.SemaphoreType.DMA((4, 4)),
-            pltpu.SemaphoreType.DMA((4, 4)),
-        ],
-        compiler_params=pltpu.CompilerParams(vmem_limit_bytes=60 * 1024 * 1024),
+        scratch_shapes=[pltpu.SemaphoreType.DMA((4, 4))],
+        compiler_params=PARAMS,
         name="gather",
     )(sections)
     recv = lax.all_to_all(send.reshape(64, 4, 2, 8, M), ("y", "core", "zl"), 0, 0)
@@ -221,23 +225,34 @@
         name="tree",
     )(recv)
     near = lax.ppermute(total, ("zh", "zl"), [(z, 7 - z) for z in range(8)])
+    turned = pl.pallas_call(
+        prefix_kernel,
+        out_shape=jax.ShapeDtypeStruct((16, 2, M, M), F32),
+        in_specs=[VMEM_SPEC] * 3,
+        out_specs=VMEM_SPEC,
+        compiler_params=PARAMS,
+        cost_estimate=pl.CostEstimate(
+            flops=11 * 6 * 8 * M * M * M, bytes_accessed=6 * 1024 * 1024, transcendentals=0
+        ),
+        name="prefix",
+    )(recv, keep, total)
     pair = pl.pallas_call(
         pair_kernel,
         out_shape=jax.ShapeDtypeStruct((4, 2, M, M), F32),
-        in_specs=[VMEM_SPEC] * 2,
+        in_specs=[VMEM_SPEC] * 3,
         out_specs=VMEM_SPEC,
         compiler_params=PARAMS,
         name="pair",
-    )(total, near)
+    )(total, near, turned)
     mats = lax.all_to_all(pair, "x", 0, 0)
     fields = pl.pallas_call(
         fields_kernel,
         out_shape=jax.ShapeDtypeStruct((4, 8, M), F32),
-        in_specs=[SMEM_SPEC] + [VMEM_SPEC] * 5,
+        in_specs=[SMEM_SPEC] + [VMEM_SPEC] * 3,
         out_specs=VMEM_SPEC,
         compiler_params=PARAMS,
         name="fields",
-    )(launch_mode, total, near, mats, recv, keep)
+    )(launch_mode, near, mats, turned)
     returned = lax.all_to_all(fields, "zl", 0, 0)
     return pl.pallas_call(
         output_kernel,

time: 107 us -> 105 us (0.981)
  Pallas kernels: 6.7 us -> 4.61 us
  local copies, waits for them, and re-layouts: 0.01 us -> 1.59 us
    pallas_call x1, Pallas kernels: 3.32 us -> 0.49 us  [shards(): pl.pallas_call(gather_kernel, out_shape=jax.ShapeDtypeStruct((16, 4, 4, 2...]
    unnamed x2 -> x4, local copies, waits for them, and re-layouts: 0.01 us -> 1.59 us
  transfers between devices with their start and end apart: 1 -> 1, of which waited for: 1 -> 1; matrix products, arithmetic and copies ran while one was open for 0% -> 0% of each run, Pallas kernels for 0% -> 1%
where the time goes in v3:
time: 105 us
  blocking collectives  84.3 us (80%)
  starting transfers between devices  8.9 us (8%)
  waiting for transfers between devices  4.95 us (5%)
  Pallas kernels  4.61 us (4%)
  local copies, waits for them, and re-layouts  1.59 us (2%)
    all_to_all x1, blocking collectives, shards(): lax.all_to_all(send.reshape(64, 4, 2, 8, M), ('y', 'core', 'zl'), 0, 0)  63.1 us
    all_to_all x1, blocking collectives, shards(): mats = lax.all_to_all(pair, 'x', 0, 0)  13.3 us
    ppermute x1, starting transfers between devices, shards(): near = lax.ppermute(total, ('zh', 'zl'), [(z, 7 - z) for z in range(8)])  8.9 us
    all_to_all x1, blocking collectives, shards(): returned = lax.all_to_all(fields, 'zl', 0, 0)  7.96 us
    ppermute x1, waiting for transfers between devices, shards(): near = lax.ppermute(total, ('zh', 'zl'), [(z, 7 - z) for z in range(8)])  4.95 us
  transfers between devices with their start and end apart: 1, of which 1 were waited for; matrix products, arithmetic and copies ran while one was open for 0% of the time, Pallas kernels for 1%

profile of v3, /device:TPU:8, one launch (start us, length us, event | category | flops | bytes accessed | tf_op | source)
XLA Modules:
  0.0 105.0 jit_solution(10733747279470824307)
XLA Ops:
  0.6 0.0 copy-start
  0.6 1.6 %copy-done = f32[4,32,2,2,8,128]{5,4,3,2,1,0:T(8,128)S(1)} copy-done((f32[4,32,2,2,8,128]{5,4,3,2,1,0:T(8,128)S(1)}, f32[4,32,2,2,8,128]{5,4,3,2,1,0:T(8,128)}, u32[]{:S(2)}) %copy-start) | copy-done | bytes 2097176
  2.2 0.5 gather.1
  2.7 63.1 %all_to_all.15 = f32[64,4,2,8,128]{4,3,2,1,0:T(8,128)S(1)} all-to-all(f32[64,4,2,8,128]{4,3,2,1,0:T(8,128)S(1)} %bitcast.5), channel_id=1, replica_groups=mesh['y'=8,'core'=2,'x'=4,'zh'=2,'zl'=4] {'y','core','zl'}, dimensions={0} | all-to-all | bytes 4194304 | tf_op jit(solution)/shard_map/all_to_all | solution.py:214
  65.8 1.2 %tree.1 = (f32[2,128,128]{2,1,0:T(8,128)S(1)}, f32[7,2,128,128]{3,2,1,0:T(8,128)S(1)}) custom-call(f32[16,4,4,2,8,128]{5,4,3,2,1,0:T(8,128)S(1)} %bitcast.3), custom_call_target="tpu_custom_call" | custom-call | tf_op jit(solution)/shard_map/tree/pallas_call | solution.py:216
  67.0 8.9 %collective-permute-start = (f32[2,128,128]{2,1,0:T(8,128)S(1)}, f32[2,128,128]{2,1,0:T(8,128)S(1)}, u32[]{:S(2)}, u32[]{:S(2)}) collective-permute-start(f32[2,128,128]{2,1,0:T(8,128)S(1)} %get-tuple-element.4.total.own), channel_id=1, source_target_pairs={{0,7},{1,6},{2,5},{3,4},{4,3},{5,2},{6,1},{7,0},{8,15},{9,14},{10,... | collective-permute-start | bytes 393224 | tf_op jit(solution)/shard_map/ppermute | solution.py:227
  75.9 1.0 prefix.1.turned
  76.9 0.0 copy-start.1
  76.9 4.9 %collective-permute-done.near = f32[2,128,128]{2,1,0:T(8,128)S(1)} collective-permute-done((f32[2,128,128]{2,1,0:T(8,128)S(1)}, f32[2,128,128]{2,1,0:T(8,128)S(1)}, u32[]{:S(2)}, u32[]{:S(2)}) %collective-permute-start) | collective-permute-done | bytes 131104 | tf_op jit(solution)/shard_map/ppermute | solution.py:227
  81.9 0.2 pair.1
  82.1 13.3 %all_to_all.16.mats = f32[4,2,128,128]{3,2,1,0:T(8,128)S(1)} all-to-all(f32[4,2,128,128]{3,2,1,0:T(8,128)S(1)} %pair.1), channel_id=1, replica_groups=mesh['y'=8,'core'=2,'x'=4,'zh'=2,'zl'=4] {'x'}, dimensions={0} | all-to-all | bytes 1048576 | tf_op jit(solution)/shard_map/all_to_all | solution.py:247
  95.4 0.0 copy-done.1
  95.4 1.1 %fields.1 = f32[4,8,128]{2,1,0:T(8,128)S(1)} custom-call(s32[2]{0:T(128)S(1)} %copy-done.1, f32[2,128,128]{2,1,0:T(8,128)S(1)} %collective-permute-done.near, f32[4,2,128,128]{3,2,1,0:T(8,128)S(1)} %all_to_all.16.mats, f32[16,2,128,128]{3,2,1,0:T(8,128)S(1)} %prefix.1.turned), custom_call_target="tpu_custom_call" | custom-call | tf_op jit(solution)/shard_map/fields/pallas_call | solution.py:248
  96.5 8.0 %all_to_all.17.returned = f32[4,8,128]{2,1,0:T(8,128)S(1)} all-to-all(f32[4,8,128]{2,1,0:T(8,128)S(1)} %fields.1), channel_id=1, replica_groups=mesh['y'=8,'core'=2,'x'=4,'zh'=2,'zl'=4] {'zl'}, dimensions={0} | all-to-all | bytes 32768 | tf_op jit(solution)/shard_map/all_to_all | solution.py:256
  104.4 0.6 outputs.1
Async XLA Ops:
  0.6 1.6 %copy-start = (f32[4,32,2,2,8,128]{5,4,3,2,1,0:T(8,128)S(1)}, f32[4,32,2,2,8,128]{5,4,3,2,1,0:T(8,128)}, u32[]{:S(2)}) copy-start(f32[4,32,2,2,8,128]{5,4,3,2,1,0:T(8,128)} %param.2) | copy-start | bytes 6291460
  67.0 14.8 %collective-permute-start = (f32[2,128,128]{2,1,0:T(8,128)S(1)}, f32[2,128,128]{2,1,0:T(8,128)S(1)}, u32[]{:S(2)}, u32[]{:S(2)}) collective-permute-start(f32[2,128,128]{2,1,0:T(8,128)S(1)} %get-tuple-element.4.total.own), channel_id=1, source_target_pairs={{0,7},{1,6},{2,5},{3,4},{4,3},{5,2},{6,1},{7,0},{8,15},{9,14},{10,... | collective-permute-start | bytes 393224 | tf_op jit(solution)/shard_map/ppermute | solution.py:227
  76.9 18.5 %copy-start.1 = (s32[2]{0:T(128)S(1)}, s32[2]{0:T(128)}, u32[]{:S(2)}) copy-start(s32[2]{0:T(128)} %mode.1) | copy-start | bytes 28

commit v4 on v3

--- a/solution.py
+++ b/solution.py
@@ -17,7 +17,7 @@
 
 
 def slot_of(zh, zl):
-    return jnp.where(zh == 0, zl, 3 - zl)
+    return zl ^ (2 * zh)
 
 
 def place():
@@ -140,9 +140,14 @@
     prefix[14] = product(kept(3), prefix[12])
     for step in range(2, 16, 2):
         prefix[step + 1] = product(section(step), prefix[step])
-    for step in range(1, 17):
+    eye = jnp.where(diagonal(), 1.0, 0.0)
+    prefix[0] = (eye, jnp.zeros_like(eye))
+    flat = {step: tuple(part.T for part in prefix[step]) for step in range(17)}
+    for index in range(16):
         for part in range(2):
-            turned[step - 1, part] = prefix[step][part].T
+            turned[index, part] = jnp.where(
+                direction == 0, flat[index + 1][part], flat[15 - index][part]
+            )
 
 
 def pair_kernel(own, near, turned, pair):
@@ -175,20 +180,15 @@
     real, imag = (
         jnp.sum(jnp.where(eye, entering[part], 0.0), axis=1, keepdims=True) for part in range(2)
     )
-    states = [entering]
-    for step in range(16):
-        mat_real, mat_imag = turned[step, 0], turned[step, 1]
-        states.append(
-            (
-                jnp.sum(mat_real * real - mat_imag * imag, axis=0, keepdims=True),
-                jnp.sum(mat_real * imag + mat_imag * real, axis=0, keepdims=True),
-            )
+    for index in range(16):
+        mat_real, mat_imag = turned[index, 0], turned[index, 1]
+        row = 2 * (index % 4)
+        out[index // 4, row : row + 1] = jnp.sum(
+            mat_real * real - mat_imag * imag, axis=0, keepdims=True
         )
-    for index in range(16):
-        for part in range(2):
-            out[index // 4, 2 * (index % 4) + part : 2 * (index % 4) + part + 1] = jnp.where(
-                direction == 0, states[index + 1][part], states[15 - index][part]
-            )
+        out[index // 4, row + 1 : row + 2] = jnp.sum(
+            mat_real * imag + mat_imag * real, axis=0, keepdims=True
+        )
 
 
 def output_kernel(returned, forward, backward):
@@ -224,7 +224,7 @@
         compiler_params=PARAMS,
         name="tree",
     )(recv)
-    near = lax.ppermute(total, ("zh", "zl"), [(z, 7 - z) for z in range(8)])
+    near = lax.ppermute(total, ("zh", "zl"), [(z, z ^ 6) for z in range(8)])
     turned = pl.pallas_call(
         prefix_kernel,
         out_shape=jax.ShapeDtypeStruct((16, 2, M, M), F32),

time: 105 us -> 106 us (level)
  no operation moved by 1% of the time
where the time goes in v4:
time: 106 us
  blocking collectives  85.2 us (80%)
  starting transfers between devices  8.89 us (8%)
  waiting for transfers between devices  4.69 us (4%)
  Pallas kernels  4.61 us (4%)
  local copies, waits for them, and re-layouts  1.59 us (2%)
    all_to_all x1, blocking collectives, shards(): lax.all_to_all(send.reshape(64, 4, 2, 8, M), ('y', 'core', 'zl'), 0, 0)  63.1 us
    all_to_all x1, blocking collectives, shards(): mats = lax.all_to_all(pair, 'x', 0, 0)  13.3 us
    ppermute x1, starting transfers between devices, shards(): near = lax.ppermute(total, ('zh', 'zl'), [(z, z ^ 6) for z in range(8)])  8.89 us
    all_to_all x1, blocking collectives, shards(): returned = lax.all_to_all(fields, 'zl', 0, 0)  8.78 us
    ppermute x1, waiting for transfers between devices, shards(): near = lax.ppermute(total, ('zh', 'zl'), [(z, z ^ 6) for z in range(8)])  4.69 us
  transfers between devices with their start and end apart: 1, of which 1 were waited for; matrix products, arithmetic and copies ran while one was open for 0% of the time, Pallas kernels for 1%

profile of v4, /device:TPU:8, one launch (start us, length us, event | category | flops | bytes accessed | tf_op | source)
XLA Modules:
  0.0 105.7 jit_solution(3421800656162419456)
XLA Ops:
  0.6 0.0 copy-start
  0.6 1.6 %copy-done = f32[4,32,2,2,8,128]{5,4,3,2,1,0:T(8,128)S(1)} copy-done((f32[4,32,2,2,8,128]{5,4,3,2,1,0:T(8,128)S(1)}, f32[4,32,2,2,8,128]{5,4,3,2,1,0:T(8,128)}, u32[]{:S(2)}) %copy-start) | copy-done | bytes 2097176
  2.2 0.5 gather.1
  2.7 63.1 %all_to_all.15 = f32[64,4,2,8,128]{4,3,2,1,0:T(8,128)S(1)} all-to-all(f32[64,4,2,8,128]{4,3,2,1,0:T(8,128)S(1)} %bitcast.5), channel_id=1, replica_groups=mesh['y'=8,'core'=2,'x'=4,'zh'=2,'zl'=4] {'y','core','zl'}, dimensions={0} | all-to-all | bytes 4194304 | tf_op jit(solution)/shard_map/all_to_all | solution.py:214
  65.8 1.2 %tree.1 = (f32[2,128,128]{2,1,0:T(8,128)S(1)}, f32[7,2,128,128]{3,2,1,0:T(8,128)S(1)}) custom-call(f32[16,4,4,2,8,128]{5,4,3,2,1,0:T(8,128)S(1)} %bitcast.3), custom_call_target="tpu_custom_call" | custom-call | tf_op jit(solution)/shard_map/tree/pallas_call | solution.py:216
  67.0 8.9 %collective-permute-start = (f32[2,128,128]{2,1,0:T(8,128)S(1)}, f32[2,128,128]{2,1,0:T(8,128)S(1)}, u32[]{:S(2)}, u32[]{:S(2)}) collective-permute-start(f32[2,128,128]{2,1,0:T(8,128)S(1)} %get-tuple-element.4.total.own), channel_id=1, source_target_pairs={{0,6},{1,7},{2,4},{3,5},{4,2},{5,3},{6,0},{7,1},{8,14},{9,15},{10,... | collective-permute-start | bytes 393224 | tf_op jit(solution)/shard_map/ppermute | solution.py:227
  75.9 1.0 prefix.1.turned
  76.9 0.0 copy-start.1
  76.9 4.7 %collective-permute-done.near = f32[2,128,128]{2,1,0:T(8,128)S(1)} collective-permute-done((f32[2,128,128]{2,1,0:T(8,128)S(1)}, f32[2,128,128]{2,1,0:T(8,128)S(1)}, u32[]{:S(2)}, u32[]{:S(2)}) %collective-permute-start) | collective-permute-done | bytes 131104 | tf_op jit(solution)/shard_map/ppermute | solution.py:227
  81.6 0.2 pair.1
  81.9 13.3 %all_to_all.16.mats = f32[4,2,128,128]{3,2,1,0:T(8,128)S(1)} all-to-all(f32[4,2,128,128]{3,2,1,0:T(8,128)S(1)} %pair.1), channel_id=1, replica_groups=mesh['y'=8,'core'=2,'x'=4,'zh'=2,'zl'=4] {'x'}, dimensions={0} | all-to-all | bytes 1048576 | tf_op jit(solution)/shard_map/all_to_all | solution.py:247
  95.2 0.0 copy-done.1
  95.2 1.1 %fields.1 = f32[4,8,128]{2,1,0:T(8,128)S(1)} custom-call(s32[2]{0:T(128)S(1)} %copy-done.1, f32[2,128,128]{2,1,0:T(8,128)S(1)} %collective-permute-done.near, f32[4,2,128,128]{3,2,1,0:T(8,128)S(1)} %all_to_all.16.mats, f32[16,2,128,128]{3,2,1,0:T(8,128)S(1)} %prefix.1.turned), custom_call_target="tpu_custom_call" | custom-call | tf_op jit(solution)/shard_map/fields/pallas_call | solution.py:248
  96.3 8.8 %all_to_all.17.returned = f32[4,8,128]{2,1,0:T(8,128)S(1)} all-to-all(f32[4,8,128]{2,1,0:T(8,128)S(1)} %fields.1), channel_id=1, replica_groups=mesh['y'=8,'core'=2,'x'=4,'zh'=2,'zl'=4] {'zl'}, dimensions={0} | all-to-all | bytes 32768 | tf_op jit(solution)/shard_map/all_to_all | solution.py:256
  105.1 0.6 outputs.1
Async XLA Ops:
  0.6 1.6 %copy-start = (f32[4,32,2,2,8,128]{5,4,3,2,1,0:T(8,128)S(1)}, f32[4,32,2,2,8,128]{5,4,3,2,1,0:T(8,128)}, u32[]{:S(2)}) copy-start(f32[4,32,2,2,8,128]{5,4,3,2,1,0:T(8,128)} %param.2) | copy-start | bytes 6291460
  67.0 14.6 %collective-permute-start = (f32[2,128,128]{2,1,0:T(8,128)S(1)}, f32[2,128,128]{2,1,0:T(8,128)S(1)}, u32[]{:S(2)}, u32[]{:S(2)}) collective-permute-start(f32[2,128,128]{2,1,0:T(8,128)S(1)} %get-tuple-element.4.total.own), channel_id=1, source_target_pairs={{0,6},{1,7},{2,4},{3,5},{4,2},{5,3},{6,0},{7,1},{8,14},{9,15},{10,... | collective-permute-start | bytes 393224 | tf_op jit(solution)/shard_map/ppermute | solution.py:227
  76.9 18.3 %copy-start.1 = (s32[2]{0:T(128)S(1)}, s32[2]{0:T(128)}, u32[]{:S(2)}) copy-start(s32[2]{0:T(128)} %mode.1) | copy-start | bytes 28

commit v5 on v4

--- a/solution.py
+++ b/solution.py
@@ -17,7 +17,7 @@
 
 
 def slot_of(zh, zl):
-    return zl ^ (2 * zh)
+    return zl ^ (3 - 3 * zh)
 
 
 def place():
@@ -31,15 +31,28 @@
 
 def gather_kernel(sections, out, sem):
     zh = lax.axis_index("zh")
-    copies = []
-    for zl in range(4):
-        slot = slot_of(zh, zl)
-        for c in range(4):
-            copy = pltpu.make_async_copy(sections.at[c, :, slot], out.at[:, zl, c], sem.at[zl, c])
+
+    @pl.when(zh == 1)
+    def _():
+        copies = [
+            pltpu.make_async_copy(sections.at[c], out.at[:, :, c], sem.at[0, c]) for c in range(4)
+        ]
+        for copy in copies:
             copy.start()
-            copies.append(copy)
-    for copy in copies:
-        copy.wait()
+        for copy in copies:
+            copy.wait()
+
+    @pl.when(zh == 0)
+    def _():
+        copies = [
+            pltpu.make_async_copy(sections.at[c, :, 3 - zl], out.at[:, zl, c], sem.at[zl, c])
+            for zl in range(4)
+            for c in range(4)
+        ]
+        for copy in copies:
+            copy.start()
+        for copy in copies:
+            copy.wait()
 
 
 def split(value):
@@ -224,7 +237,7 @@
         compiler_params=PARAMS,
         name="tree",
     )(recv)
-    near = lax.ppermute(total, ("zh", "zl"), [(z, z ^ 6) for z in range(8)])
+    near = lax.ppermute(total, ("zh", "zl"), [(z, z ^ 7) for z in range(8)])
     turned = pl.pallas_call(
         prefix_kernel,
         out_shape=jax.ShapeDtypeStruct((16, 2, M, M), F32),

time: 106 us -> 106 us (level)
  no operation moved by 1% of the time
where the time goes in v5:
time: 106 us; the launch traced here: 105 us
  blocking collectives  84.3 us (80%)
  starting transfers between devices  8.87 us (8%)
  Pallas kernels  5.09 us (5%)
  waiting for transfers between devices  4.92 us (5%)
  local copies, waits for them, and re-layouts  1.59 us (2%)
    all_to_all x1, blocking collectives, shards(): lax.all_to_all(send.reshape(64, 4, 2, 8, M), ('y', 'core', 'zl'), 0, 0)  63.1 us
    all_to_all x1, blocking collectives, shards(): mats = lax.all_to_all(pair, 'x', 0, 0)  13.3 us
    ppermute x1, starting transfers between devices, shards(): near = lax.ppermute(total, ('zh', 'zl'), [(z, z ^ 7) for z in range(8)])  8.87 us
    all_to_all x1, blocking collectives, shards(): returned = lax.all_to_all(fields, 'zl', 0, 0)  7.96 us
    ppermute x1, waiting for transfers between devices, shards(): near = lax.ppermute(total, ('zh', 'zl'), [(z, z ^ 7) for z in range(8)])  4.92 us
  transfers between devices with their start and end apart: 1, of which 1 were waited for; matrix products, arithmetic and copies ran while one was open for 0% of the time, Pallas kernels for 1%

profile of v5, /device:TPU:8, one launch (start us, length us, event | category | flops | bytes accessed | tf_op | source)
XLA Modules:
  0.0 105.5 jit_solution(13088136710101936891)
XLA Ops:
  0.6 0.0 copy-start
  0.6 1.6 %copy-done = f32[4,32,2,2,8,128]{5,4,3,2,1,0:T(8,128)S(1)} copy-done((f32[4,32,2,2,8,128]{5,4,3,2,1,0:T(8,128)S(1)}, f32[4,32,2,2,8,128]{5,4,3,2,1,0:T(8,128)}, u32[]{:S(2)}) %copy-start) | copy-done | bytes 2097176
  2.2 0.5 gather.1
  2.7 63.1 %all_to_all.15 = f32[64,4,2,8,128]{4,3,2,1,0:T(8,128)S(1)} all-to-all(f32[64,4,2,8,128]{4,3,2,1,0:T(8,128)S(1)} %bitcast.5), channel_id=1, replica_groups=mesh['y'=8,'core'=2,'x'=4,'zh'=2,'zl'=4] {'y','core','zl'}, dimensions={0} | all-to-all | bytes 4194304 | tf_op jit(solution)/shard_map/all_to_all | solution.py:227
  65.8 1.2 %tree.1 = (f32[2,128,128]{2,1,0:T(8,128)S(1)}, f32[7,2,128,128]{3,2,1,0:T(8,128)S(1)}) custom-call(f32[16,4,4,2,8,128]{5,4,3,2,1,0:T(8,128)S(1)} %bitcast.3), custom_call_target="tpu_custom_call" | custom-call | tf_op jit(solution)/shard_map/tree/pallas_call | solution.py:229
  67.0 8.9 %collective-permute-start = (f32[2,128,128]{2,1,0:T(8,128)S(1)}, f32[2,128,128]{2,1,0:T(8,128)S(1)}, u32[]{:S(2)}, u32[]{:S(2)}) collective-permute-start(f32[2,128,128]{2,1,0:T(8,128)S(1)} %get-tuple-element.4.total.own), channel_id=1, source_target_pairs={{0,7},{1,6},{2,5},{3,4},{4,3},{5,2},{6,1},{7,0},{8,15},{9,14},{10,... | collective-permute-start | bytes 393224 | tf_op jit(solution)/shard_map/ppermute | solution.py:240
  75.9 1.0 prefix.1.turned
  76.9 0.0 copy-start.1
  76.9 4.9 %collective-permute-done.near = f32[2,128,128]{2,1,0:T(8,128)S(1)} collective-permute-done((f32[2,128,128]{2,1,0:T(8,128)S(1)}, f32[2,128,128]{2,1,0:T(8,128)S(1)}, u32[]{:S(2)}, u32[]{:S(2)}) %collective-permute-start) | collective-permute-done | bytes 131104 | tf_op jit(solution)/shard_map/ppermute | solution.py:240
  81.8 0.2 pair.1
  82.1 13.3 %all_to_all.16.mats = f32[4,2,128,128]{3,2,1,0:T(8,128)S(1)} all-to-all(f32[4,2,128,128]{3,2,1,0:T(8,128)S(1)} %pair.1), channel_id=1, replica_groups=mesh['y'=8,'core'=2,'x'=4,'zh'=2,'zl'=4] {'x'}, dimensions={0} | all-to-all | bytes 1048576 | tf_op jit(solution)/shard_map/all_to_all | solution.py:260
  95.4 0.0 copy-done.1
  95.4 1.5 %fields.1 = f32[4,8,128]{2,1,0:T(8,128)S(1)} custom-call(s32[2]{0:T(128)S(1)} %copy-done.1, f32[2,128,128]{2,1,0:T(8,128)S(1)} %collective-permute-done.near, f32[4,2,128,128]{3,2,1,0:T(8,128)S(1)} %all_to_all.16.mats, f32[16,2,128,128]{3,2,1,0:T(8,128)S(1)} %prefix.1.turned), custom_call_target="tpu_custom_call" | custom-call | tf_op jit(solution)/shard_map/fields/pallas_call | solution.py:261
  96.9 8.0 %all_to_all.17.returned = f32[4,8,128]{2,1,0:T(8,128)S(1)} all-to-all(f32[4,8,128]{2,1,0:T(8,128)S(1)} %fields.1), channel_id=1, replica_groups=mesh['y'=8,'core'=2,'x'=4,'zh'=2,'zl'=4] {'zl'}, dimensions={0} | all-to-all | bytes 32768 | tf_op jit(solution)/shard_map/all_to_all | solution.py:269
  104.9 0.6 outputs.1
Async XLA Ops:
  0.6 1.6 %copy-start = (f32[4,32,2,2,8,128]{5,4,3,2,1,0:T(8,128)S(1)}, f32[4,32,2,2,8,128]{5,4,3,2,1,0:T(8,128)}, u32[]{:S(2)}) copy-start(f32[4,32,2,2,8,128]{5,4,3,2,1,0:T(8,128)} %param.2) | copy-start | bytes 6291460
  67.0 14.8 %collective-permute-start = (f32[2,128,128]{2,1,0:T(8,128)S(1)}, f32[2,128,128]{2,1,0:T(8,128)S(1)}, u32[]{:S(2)}, u32[]{:S(2)}) collective-permute-start(f32[2,128,128]{2,1,0:T(8,128)S(1)} %get-tuple-element.4.total.own), channel_id=1, source_target_pairs={{0,7},{1,6},{2,5},{3,4},{4,3},{5,2},{6,1},{7,0},{8,15},{9,14},{10,... | collective-permute-start | bytes 393224 | tf_op jit(solution)/shard_map/ppermute | solution.py:240
  76.9 18.5 %copy-start.1 = (s32[2]{0:T(128)S(1)}, s32[2]{0:T(128)}, u32[]{:S(2)}) copy-start(s32[2]{0:T(128)} %mode.1) | copy-start | bytes 28

commit v6 on v3

--- a/solution.py
+++ b/solution.py
@@ -35,7 +35,9 @@
     for zl in range(4):
         slot = slot_of(zh, zl)
         for c in range(4):
-            copy = pltpu.make_async_copy(sections.at[c, :, slot], out.at[:, zl, c], sem.at[zl, c])
+            copy = pltpu.make_async_copy(
+                sections.at[c, :, :, slot], out.at[:, zl, :, c], sem.at[zl, c]
+            )
             copy.start()
             copies.append(copy)
     for copy in copies:
@@ -85,7 +87,7 @@
 def section_of(recv, order, step):
     index = jnp.where(order == 0, step, 15 - step)
     zl, c = index // 4, lax.rem(index, 4)
-    return tuple(recv[:, zl, c, part].reshape(M, M) for part in range(2))
+    return tuple(recv[:, zl, :, c, part].reshape(M, M) for part in range(2))
 
 
 def tree_kernel(recv, total, keep):
@@ -201,18 +203,18 @@
 
 
 def shards(sections, launch_mode):
-    sections = sections.reshape(4, 16, 4, 2, 8, M)
+    sections = sections.reshape(4, 8, 2, 4, 2, 8, M)
     send = pl.pallas_call(
         gather_kernel,
-        out_shape=jax.ShapeDtypeStruct((16, 4, 4, 2, 8, M), F32),
+        out_shape=jax.ShapeDtypeStruct((8, 4, 2, 4, 2, 8, M), F32),
         in_specs=[HBM_SPEC],
         out_specs=VMEM_SPEC,
         scratch_shapes=[pltpu.SemaphoreType.DMA((4, 4))],
         compiler_params=PARAMS,
         name="gather",
     )(sections)
-    recv = lax.all_to_all(send.reshape(64, 4, 2, 8, M), ("y", "core", "zl"), 0, 0)
-    recv = recv.reshape(16, 4, 4, 2, 8, M)
+    recv = lax.all_to_all(send.reshape(64, 4, 2, 8, M), ("y", "zl", "core"), 0, 0)
+    recv = recv.reshape(8, 4, 2, 4, 2, 8, M)
     total, keep = pl.pallas_call(
         tree_kernel,
         out_shape=(

time: 105 us -> 106 us (level)
  blocking collectives: 84.3 us -> 85.8 us
where the time goes in v6:
time: 106 us
  blocking collectives  85.8 us (81%)
  starting transfers between devices  8.26 us (8%)
  waiting for transfers between devices  4.92 us (5%)
  Pallas kernels  4.61 us (4%)
  local copies, waits for them, and re-layouts  1.59 us (2%)
    all_to_all x1, blocking collectives, shards(): lax.all_to_all(send.reshape(64, 4, 2, 8, M), ('y', 'zl', 'core'), 0, 0)  63.7 us
    all_to_all x1, blocking collectives, shards(): mats = lax.all_to_all(pair, 'x', 0, 0)  13.7 us
    all_to_all x1, blocking collectives, shards(): returned = lax.all_to_all(fields, 'zl', 0, 0)  8.31 us
    ppermute x1, starting transfers between devices, shards(): near = lax.ppermute(total, ('zh', 'zl'), [(z, 7 - z) for z in range(8)])  8.26 us
    ppermute x1, waiting for transfers between devices, shards(): near = lax.ppermute(total, ('zh', 'zl'), [(z, 7 - z) for z in range(8)])  4.92 us
  transfers between devices with their start and end apart: 1, of which 1 were waited for; matrix products, arithmetic and copies ran while one was open for 0% of the time, Pallas kernels for 1%

profile of v6, /device:TPU:8, one launch (start us, length us, event | category | flops | bytes accessed | tf_op | source)
XLA Modules:
  0.0 105.8 jit_solution(4870377846534783472)
XLA Ops:
  0.6 0.0 copy-start
  0.6 1.6 %copy-done = f32[4,32,2,2,8,128]{5,4,3,2,1,0:T(8,128)S(1)} copy-done((f32[4,32,2,2,8,128]{5,4,3,2,1,0:T(8,128)S(1)}, f32[4,32,2,2,8,128]{5,4,3,2,1,0:T(8,128)}, u32[]{:S(2)}) %copy-start) | copy-done | bytes 2097176
  2.2 0.5 gather.1
  2.7 63.7 %all_to_all.15 = f32[64,4,2,8,128]{4,3,2,1,0:T(8,128)S(1)} all-to-all(f32[64,4,2,8,128]{4,3,2,1,0:T(8,128)S(1)} %bitcast.5), channel_id=1, replica_groups=mesh['y'=8,'core'=2,'x'=4,'zh'=2,'zl'=4] {'y','zl','core'}, dimensions={0} | all-to-all | bytes 4194304 | tf_op jit(solution)/shard_map/all_to_all | solution.py:216
  66.4 1.2 %tree.1 = (f32[2,128,128]{2,1,0:T(8,128)S(1)}, f32[7,2,128,128]{3,2,1,0:T(8,128)S(1)}) custom-call(f32[8,4,2,4,2,8,128]{6,5,4,3,2,1,0:T(8,128)S(1)} %bitcast.3), custom_call_target="tpu_custom_call" | custom-call | tf_op jit(solution)/shard_map/tree/pallas_call | solution.py:218
  67.7 8.3 %collective-permute-start = (f32[2,128,128]{2,1,0:T(8,128)S(1)}, f32[2,128,128]{2,1,0:T(8,128)S(1)}, u32[]{:S(2)}, u32[]{:S(2)}) collective-permute-start(f32[2,128,128]{2,1,0:T(8,128)S(1)} %get-tuple-element.4.total.own), channel_id=1, source_target_pairs={{0,7},{1,6},{2,5},{3,4},{4,3},{5,2},{6,1},{7,0},{8,15},{9,14},{10,... | collective-permute-start | bytes 393224 | tf_op jit(solution)/shard_map/ppermute | solution.py:229
  75.9 1.0 prefix.1.turned
  76.9 0.0 copy-start.1
  76.9 4.9 %collective-permute-done.near = f32[2,128,128]{2,1,0:T(8,128)S(1)} collective-permute-done((f32[2,128,128]{2,1,0:T(8,128)S(1)}, f32[2,128,128]{2,1,0:T(8,128)S(1)}, u32[]{:S(2)}, u32[]{:S(2)}) %collective-permute-start) | collective-permute-done | bytes 131104 | tf_op jit(solution)/shard_map/ppermute | solution.py:229
  81.8 0.2 pair.1
  82.1 13.7 %all_to_all.16.mats = f32[4,2,128,128]{3,2,1,0:T(8,128)S(1)} all-to-all(f32[4,2,128,128]{3,2,1,0:T(8,128)S(1)} %pair.1), channel_id=1, replica_groups=mesh['y'=8,'core'=2,'x'=4,'zh'=2,'zl'=4] {'x'}, dimensions={0} | all-to-all | bytes 1048576 | tf_op jit(solution)/shard_map/all_to_all | solution.py:249
  95.8 0.0 copy-done.1
  95.9 1.1 %fields.1 = f32[4,8,128]{2,1,0:T(8,128)S(1)} custom-call(s32[2]{0:T(128)S(1)} %copy-done.1, f32[2,128,128]{2,1,0:T(8,128)S(1)} %collective-permute-done.near, f32[4,2,128,128]{3,2,1,0:T(8,128)S(1)} %all_to_all.16.mats, f32[16,2,128,128]{3,2,1,0:T(8,128)S(1)} %prefix.1.turned), custom_call_target="tpu_custom_call" | custom-call | tf_op jit(solution)/shard_map/fields/pallas_call | solution.py:250
  96.9 8.3 %all_to_all.17.returned = f32[4,8,128]{2,1,0:T(8,128)S(1)} all-to-all(f32[4,8,128]{2,1,0:T(8,128)S(1)} %fields.1), channel_id=1, replica_groups=mesh['y'=8,'core'=2,'x'=4,'zh'=2,'zl'=4] {'zl'}, dimensions={0} | all-to-all | bytes 32768 | tf_op jit(solution)/shard_map/all_to_all | solution.py:258
  105.2 0.6 outputs.1
Async XLA Ops:
  0.6 1.6 %copy-start = (f32[4,32,2,2,8,128]{5,4,3,2,1,0:T(8,128)S(1)}, f32[4,32,2,2,8,128]{5,4,3,2,1,0:T(8,128)}, u32[]{:S(2)}) copy-start(f32[4,32,2,2,8,128]{5,4,3,2,1,0:T(8,128)} %param.2) | copy-start | bytes 6291460
  67.7 14.2 %collective-permute-start = (f32[2,128,128]{2,1,0:T(8,128)S(1)}, f32[2,128,128]{2,1,0:T(8,128)S(1)}, u32[]{:S(2)}, u32[]{:S(2)}) collective-permute-start(f32[2,128,128]{2,1,0:T(8,128)S(1)} %get-tuple-element.4.total.own), channel_id=1, source_target_pairs={{0,7},{1,6},{2,5},{3,4},{4,3},{5,2},{6,1},{7,0},{8,15},{9,14},{10,... | collective-permute-start | bytes 393224 | tf_op jit(solution)/shard_map/ppermute | solution.py:229
  76.9 18.9 %copy-start.1 = (s32[2]{0:T(128)S(1)}, s32[2]{0:T(128)}, u32[]{:S(2)}) copy-start(s32[2]{0:T(128)} %mode.1) | copy-start | bytes 28

commit v7 on v3

--- a/solution.py
+++ b/solution.py
@@ -105,12 +105,14 @@
 
 def matvec(mat, vec, eye):
     mat_real, mat_imag = mat
-    real, imag = vec
+    real, imag = vec[:2]
     out_real = jnp.sum(mat_real * real - mat_imag * imag, axis=1, keepdims=True)
     out_imag = jnp.sum(mat_real * imag + mat_imag * real, axis=1, keepdims=True)
     return (
         jnp.sum(jnp.where(eye, out_real, 0.0), axis=0, keepdims=True),
         jnp.sum(jnp.where(eye, out_imag, 0.0), axis=0, keepdims=True),
+        out_real,
+        out_imag,
     )
 
 
@@ -119,9 +121,12 @@
 
 
 def launch_vector(mode, b):
-    lane = lax.broadcasted_iota(jnp.int32, (1, M), 1)
-    onehot = jnp.where(lane == mode[b], jnp.float32(math.sqrt(M)), 0.0)
-    return onehot, jnp.zeros_like(onehot)
+    forms = []
+    for shape, axis in (((1, M), 1), ((M, 1), 0)):
+        index = lax.broadcasted_iota(jnp.int32, shape, axis)
+        onehot = jnp.where(index == mode[b], jnp.float32(math.sqrt(M)), 0.0)
+        forms += [onehot, jnp.zeros_like(onehot)]
+    return tuple(forms)
 
 
 def prefix_kernel(recv, keep, total, turned):
@@ -172,9 +177,7 @@
         return matvec((near[0], near[1]), vec, eye)
 
     entering = lax.fori_loop(0, lax.rem(spot, 2), step_in, vec)
-    real, imag = (
-        jnp.sum(jnp.where(eye, entering[part], 0.0), axis=1, keepdims=True) for part in range(2)
-    )
+    real, imag = entering[2:]
     states = [entering]
     for step in range(16):
         mat_real, mat_imag = turned[step, 0], turned[step, 1]

time: 105 us -> 105 us (level)
  no operation moved by 1% of the time
where the time goes in v7:
time: 105 us
  blocking collectives  84.3 us (80%)
  starting transfers between devices  8.9 us (8%)
  waiting for transfers between devices  4.95 us (5%)
  Pallas kernels  4.47 us (4%)
  local copies, waits for them, and re-layouts  1.59 us (2%)
    all_to_all x1, blocking collectives, shards(): lax.all_to_all(send.reshape(64, 4, 2, 8, M), ('y', 'core', 'zl'), 0, 0)  63.1 us
    all_to_all x1, blocking collectives, shards(): mats = lax.all_to_all(pair, 'x', 0, 0)  13.3 us
    ppermute x1, starting transfers between devices, shards(): near = lax.ppermute(total, ('zh', 'zl'), [(z, 7 - z) for z in range(8)])  8.9 us
    all_to_all x1, blocking collectives, shards(): returned = lax.all_to_all(fields, 'zl', 0, 0)  7.96 us
    ppermute x1, waiting for transfers between devices, shards(): near = lax.ppermute(total, ('zh', 'zl'), [(z, 7 - z) for z in range(8)])  4.95 us
  transfers between devices with their start and end apart: 1, of which 1 were waited for; matrix products, arithmetic and copies ran while one was open for 0% of the time, Pallas kernels for 1%

profile of v7, /device:TPU:8, one launch (start us, length us, event | category | flops | bytes accessed | tf_op | source)
XLA Modules:
  0.0 104.9 jit_solution(5216263175674909901)
XLA Ops:
  0.6 0.0 copy-start
  0.6 1.6 %copy-done = f32[4,32,2,2,8,128]{5,4,3,2,1,0:T(8,128)S(1)} copy-done((f32[4,32,2,2,8,128]{5,4,3,2,1,0:T(8,128)S(1)}, f32[4,32,2,2,8,128]{5,4,3,2,1,0:T(8,128)}, u32[]{:S(2)}) %copy-start) | copy-done | bytes 2097176
  2.2 0.5 gather.1
  2.7 63.1 %all_to_all.15 = f32[64,4,2,8,128]{4,3,2,1,0:T(8,128)S(1)} all-to-all(f32[64,4,2,8,128]{4,3,2,1,0:T(8,128)S(1)} %bitcast.5), channel_id=1, replica_groups=mesh['y'=8,'core'=2,'x'=4,'zh'=2,'zl'=4] {'y','core','zl'}, dimensions={0} | all-to-all | bytes 4194304 | tf_op jit(solution)/shard_map/all_to_all | solution.py:217
  65.8 1.2 %tree.1 = (f32[2,128,128]{2,1,0:T(8,128)S(1)}, f32[7,2,128,128]{3,2,1,0:T(8,128)S(1)}) custom-call(f32[16,4,4,2,8,128]{5,4,3,2,1,0:T(8,128)S(1)} %bitcast.3), custom_call_target="tpu_custom_call" | custom-call | tf_op jit(solution)/shard_map/tree/pallas_call | solution.py:219
  67.0 8.9 %collective-permute-start = (f32[2,128,128]{2,1,0:T(8,128)S(1)}, f32[2,128,128]{2,1,0:T(8,128)S(1)}, u32[]{:S(2)}, u32[]{:S(2)}) collective-permute-start(f32[2,128,128]{2,1,0:T(8,128)S(1)} %get-tuple-element.4.total.own), channel_id=1, source_target_pairs={{0,7},{1,6},{2,5},{3,4},{4,3},{5,2},{6,1},{7,0},{8,15},{9,14},{10,... | collective-permute-start | bytes 393224 | tf_op jit(solution)/shard_map/ppermute | solution.py:230
  75.9 1.0 prefix.1.turned
  76.9 0.0 copy-start.1
  76.9 4.9 %collective-permute-done.near = f32[2,128,128]{2,1,0:T(8,128)S(1)} collective-permute-done((f32[2,128,128]{2,1,0:T(8,128)S(1)}, f32[2,128,128]{2,1,0:T(8,128)S(1)}, u32[]{:S(2)}, u32[]{:S(2)}) %collective-permute-start) | collective-permute-done | bytes 131104 | tf_op jit(solution)/shard_map/ppermute | solution.py:230
  81.9 0.2 pair.1
  82.1 13.3 %all_to_all.16.mats = f32[4,2,128,128]{3,2,1,0:T(8,128)S(1)} all-to-all(f32[4,2,128,128]{3,2,1,0:T(8,128)S(1)} %pair.1), channel_id=1, replica_groups=mesh['y'=8,'core'=2,'x'=4,'zh'=2,'zl'=4] {'x'}, dimensions={0} | all-to-all | bytes 1048576 | tf_op jit(solution)/shard_map/all_to_all | solution.py:250
  95.4 0.0 copy-done.1
  95.4 0.9 fields.1
  96.3 8.0 %all_to_all.17.returned = f32[4,8,128]{2,1,0:T(8,128)S(1)} all-to-all(f32[4,8,128]{2,1,0:T(8,128)S(1)} %fields.1), channel_id=1, replica_groups=mesh['y'=8,'core'=2,'x'=4,'zh'=2,'zl'=4] {'zl'}, dimensions={0} | all-to-all | bytes 32768 | tf_op jit(solution)/shard_map/all_to_all | solution.py:259
  104.3 0.6 outputs.1
Async XLA Ops:
  0.6 1.6 %copy-start = (f32[4,32,2,2,8,128]{5,4,3,2,1,0:T(8,128)S(1)}, f32[4,32,2,2,8,128]{5,4,3,2,1,0:T(8,128)}, u32[]{:S(2)}) copy-start(f32[4,32,2,2,8,128]{5,4,3,2,1,0:T(8,128)} %param.2) | copy-start | bytes 6291460
  67.0 14.8 %collective-permute-start = (f32[2,128,128]{2,1,0:T(8,128)S(1)}, f32[2,128,128]{2,1,0:T(8,128)S(1)}, u32[]{:S(2)}, u32[]{:S(2)}) collective-permute-start(f32[2,128,128]{2,1,0:T(8,128)S(1)} %get-tuple-element.4.total.own), channel_id=1, source_target_pairs={{0,7},{1,6},{2,5},{3,4},{4,3},{5,2},{6,1},{7,0},{8,15},{9,14},{10,... | collective-permute-start | bytes 393224 | tf_op jit(solution)/shard_map/ppermute | solution.py:230
  76.9 18.5 %copy-start.1 = (s32[2]{0:T(128)S(1)}, s32[2]{0:T(128)}, u32[]{:S(2)}) copy-start(s32[2]{0:T(128)} %mode.1) | copy-start | bytes 28

commit v8 on v4

--- a/solution.py
+++ b/solution.py
@@ -17,7 +17,7 @@
 
 
 def slot_of(zh, zl):
-    return zl ^ (2 * zh)
+    return jnp.where(zh == 0, zl, 3 - zl)
 
 
 def place():
@@ -105,12 +105,14 @@
 
 def matvec(mat, vec, eye):
     mat_real, mat_imag = mat
-    real, imag = vec
+    real, imag = vec[:2]
     out_real = jnp.sum(mat_real * real - mat_imag * imag, axis=1, keepdims=True)
     out_imag = jnp.sum(mat_real * imag + mat_imag * real, axis=1, keepdims=True)
     return (
         jnp.sum(jnp.where(eye, out_real, 0.0), axis=0, keepdims=True),
         jnp.sum(jnp.where(eye, out_imag, 0.0), axis=0, keepdims=True),
+        out_real,
+        out_imag,
     )
 
 
@@ -119,9 +121,12 @@
 
 
 def launch_vector(mode, b):
-    lane = lax.broadcasted_iota(jnp.int32, (1, M), 1)
-    onehot = jnp.where(lane == mode[b], jnp.float32(math.sqrt(M)), 0.0)
-    return onehot, jnp.zeros_like(onehot)
+    forms = []
+    for shape, axis in (((1, M), 1), ((M, 1), 0)):
+        index = lax.broadcasted_iota(jnp.int32, shape, axis)
+        onehot = jnp.where(index == mode[b], jnp.float32(math.sqrt(M)), 0.0)
+        forms += [onehot, jnp.zeros_like(onehot)]
+    return tuple(forms)
 
 
 def prefix_kernel(recv, keep, total, turned):
@@ -177,9 +182,7 @@
         return matvec((near[0], near[1]), vec, eye)
 
     entering = lax.fori_loop(0, lax.rem(spot, 2), step_in, vec)
-    real, imag = (
-        jnp.sum(jnp.where(eye, entering[part], 0.0), axis=1, keepdims=True) for part in range(2)
-    )
+    real, imag = entering[2:]
     for index in range(16):
         mat_real, mat_imag = turned[index, 0], turned[index, 1]
         row = 2 * (index % 4)
@@ -224,7 +227,7 @@
         compiler_params=PARAMS,
         name="tree",
     )(recv)
-    near = lax.ppermute(total, ("zh", "zl"), [(z, z ^ 6) for z in range(8)])
+    near = lax.ppermute(total, ("zh", "zl"), [(z, 7 - z) for z in range(8)])
     turned = pl.pallas_call(
         prefix_kernel,
         out_shape=jax.ShapeDtypeStruct((16, 2, M, M), F32),

time: 106 us -> 105 us (level)
  no operation moved by 1% of the time
where the time goes in v8:
time: 105 us
  blocking collectives  84.3 us (80%)
  starting transfers between devices  8.9 us (8%)
  waiting for transfers between devices  4.94 us (5%)
  Pallas kernels  4.44 us (4%)
  local copies, waits for them, and re-layouts  1.59 us (2%)
    all_to_all x1, blocking collectives, shards(): lax.all_to_all(send.reshape(64, 4, 2, 8, M), ('y', 'core', 'zl'), 0, 0)  63.1 us
    all_to_all x1, blocking collectives, shards(): mats = lax.all_to_all(pair, 'x', 0, 0)  13.3 us
    ppermute x1, starting transfers between devices, shards(): near = lax.ppermute(total, ('zh', 'zl'), [(z, 7 - z) for z in range(8)])  8.9 us
    all_to_all x1, blocking collectives, shards(): returned = lax.all_to_all(fields, 'zl', 0, 0)  7.96 us
    ppermute x1, waiting for transfers between devices, shards(): near = lax.ppermute(total, ('zh', 'zl'), [(z, 7 - z) for z in range(8)])  4.94 us
  transfers between devices with their start and end apart: 1, of which 1 were waited for; matrix products, arithmetic and copies ran while one was open for 0% of the time, Pallas kernels for 1%

profile of v8, /device:TPU:8, one launch (start us, length us, event | category | flops | bytes accessed | tf_op | source)
XLA Modules:
  0.0 104.9 jit_solution(3034993647407288784)
XLA Ops:
  0.6 0.0 copy-start
  0.6 1.6 %copy-done = f32[4,32,2,2,8,128]{5,4,3,2,1,0:T(8,128)S(1)} copy-done((f32[4,32,2,2,8,128]{5,4,3,2,1,0:T(8,128)S(1)}, f32[4,32,2,2,8,128]{5,4,3,2,1,0:T(8,128)}, u32[]{:S(2)}) %copy-start) | copy-done | bytes 2097176
  2.2 0.5 gather.1
  2.7 63.1 %all_to_all.15 = f32[64,4,2,8,128]{4,3,2,1,0:T(8,128)S(1)} all-to-all(f32[64,4,2,8,128]{4,3,2,1,0:T(8,128)S(1)} %bitcast.5), channel_id=1, replica_groups=mesh['y'=8,'core'=2,'x'=4,'zh'=2,'zl'=4] {'y','core','zl'}, dimensions={0} | all-to-all | bytes 4194304 | tf_op jit(solution)/shard_map/all_to_all | solution.py:217
  65.8 1.2 %tree.1 = (f32[2,128,128]{2,1,0:T(8,128)S(1)}, f32[7,2,128,128]{3,2,1,0:T(8,128)S(1)}) custom-call(f32[16,4,4,2,8,128]{5,4,3,2,1,0:T(8,128)S(1)} %bitcast.3), custom_call_target="tpu_custom_call" | custom-call | tf_op jit(solution)/shard_map/tree/pallas_call | solution.py:219
  67.0 8.9 %collective-permute-start = (f32[2,128,128]{2,1,0:T(8,128)S(1)}, f32[2,128,128]{2,1,0:T(8,128)S(1)}, u32[]{:S(2)}, u32[]{:S(2)}) collective-permute-start(f32[2,128,128]{2,1,0:T(8,128)S(1)} %get-tuple-element.4.total.own), channel_id=1, source_target_pairs={{0,7},{1,6},{2,5},{3,4},{4,3},{5,2},{6,1},{7,0},{8,15},{9,14},{10,... | collective-permute-start | bytes 393224 | tf_op jit(solution)/shard_map/ppermute | solution.py:230
  75.9 1.0 prefix.1.turned
  76.9 0.0 copy-start.1
  76.9 4.9 %collective-permute-done.near = f32[2,128,128]{2,1,0:T(8,128)S(1)} collective-permute-done((f32[2,128,128]{2,1,0:T(8,128)S(1)}, f32[2,128,128]{2,1,0:T(8,128)S(1)}, u32[]{:S(2)}, u32[]{:S(2)}) %collective-permute-start) | collective-permute-done | bytes 131104 | tf_op jit(solution)/shard_map/ppermute | solution.py:230
  81.9 0.2 pair.1
  82.1 13.3 %all_to_all.16.mats = f32[4,2,128,128]{3,2,1,0:T(8,128)S(1)} all-to-all(f32[4,2,128,128]{3,2,1,0:T(8,128)S(1)} %pair.1), channel_id=1, replica_groups=mesh['y'=8,'core'=2,'x'=4,'zh'=2,'zl'=4] {'x'}, dimensions={0} | all-to-all | bytes 1048576 | tf_op jit(solution)/shard_map/all_to_all | solution.py:250
  95.4 0.0 copy-done.1
  95.4 0.9 fields.1
  96.3 8.0 %all_to_all.17.returned = f32[4,8,128]{2,1,0:T(8,128)S(1)} all-to-all(f32[4,8,128]{2,1,0:T(8,128)S(1)} %fields.1), channel_id=1, replica_groups=mesh['y'=8,'core'=2,'x'=4,'zh'=2,'zl'=4] {'zl'}, dimensions={0} | all-to-all | bytes 32768 | tf_op jit(solution)/shard_map/all_to_all | solution.py:259
  104.3 0.6 outputs.1
Async XLA Ops:
  0.6 1.6 %copy-start = (f32[4,32,2,2,8,128]{5,4,3,2,1,0:T(8,128)S(1)}, f32[4,32,2,2,8,128]{5,4,3,2,1,0:T(8,128)}, u32[]{:S(2)}) copy-start(f32[4,32,2,2,8,128]{5,4,3,2,1,0:T(8,128)} %param.2) | copy-start | bytes 6291460
  67.0 14.8 %collective-permute-start = (f32[2,128,128]{2,1,0:T(8,128)S(1)}, f32[2,128,128]{2,1,0:T(8,128)S(1)}, u32[]{:S(2)}, u32[]{:S(2)}) collective-permute-start(f32[2,128,128]{2,1,0:T(8,128)S(1)} %get-tuple-element.4.total.own), channel_id=1, source_target_pairs={{0,7},{1,6},{2,5},{3,4},{4,3},{5,2},{6,1},{7,0},{8,15},{9,14},{10,... | collective-permute-start | bytes 393224 | tf_op jit(solution)/shard_map/ppermute | solution.py:230
  76.9 18.5 %copy-start.1 = (s32[2]{0:T(128)S(1)}, s32[2]{0:T(128)}, u32[]{:S(2)}) copy-start(s32[2]{0:T(128)} %mode.1) | copy-start | bytes 28
